TPU v7x, 32 devices: a whole 2x2x4 slice. The times are simulated.
32 devices in a mesh: dp: 8 (over z, y), grad: 4 (over x, core).
Axes of the slice: x: 2, y: 2, z: 4, core: 2. Of those that a mesh axis runs over, the one named last changes fastest.
Arguments:
- activations: bfloat16 [2048, 5120], P('dp', 'grad')
- grad_rows: bfloat16 [41472, 5120], P(('grad', 'dp')), may hold values from -6 to 6
- live_rows: int32 [4], P('grad'), may hold values from 1 to 10368, 27648 in all
Outputs:
- preconditioned: float32 [41472, 5120], P(('grad', 'dp'))
Inputs may be any that keep to these rules, and one draw needn't show every extreme that they name: `live_rows`: the counts sum to 27648, and one worker's count is exactly 10368.
All inputs are finite; a program needn't handle non-finite values. No bound on the sum of `live_rows` on one device may be relied on, other than what follows from the above.
Results may differ from a plain program's by a relative error of at most 0.0003.
Values sent between devices are 32-bit elements; how exact they have to be, the bound alone decides.
No kernel may reach another device: no remote copies, remote signals or barrier semaphores. Data moves between devices by JAX's collectives and lax.ppermute only.
A program may use at most 128 MiB of HBM per device.

v0:
```python
import jax
import jax.numpy as jnp
from jax import lax
from jax.sharding import PartitionSpec as P

D = 5120
BLK = 160


def invert_damped(statistics, level, identity):
    factors = jnp.linalg.cholesky(statistics + level * identity)
    lower_inv = lax.linalg.triangular_solve(
        factors, jnp.broadcast_to(identity, factors.shape), left_side=True, lower=True
    )
    return jnp.einsum("kji,kjl->kil", lower_inv, lower_inv, precision=lax.Precision.HIGHEST)


def shards(activations, grad_rows, live_rows):
    count_tokens = activations.shape[0]
    col_blocks = activations.shape[1] // BLK
    total_tokens = count_tokens * lax.axis_size("dp")
    blocks = activations.reshape(count_tokens, col_blocks, BLK)
    partial_value = lax.dot_general(
        blocks, blocks, (((0,), (0,)), ((1,), (1,))), preferred_element_type=jnp.float32
    )
    partial_value = partial_value * (1.0 / total_tokens)
    identity = jnp.eye(BLK, dtype=jnp.float32)[None, :, :]
    diag_part = jnp.sum(jnp.diagonal(partial_value, axis1=1, axis2=2))
    statistics, column_trace = lax.psum((partial_value, diag_part), "dp")
    diag_total = lax.psum(column_trace, "grad")
    level = 0.5 * diag_total / D + 1e-06
    owned = invert_damped(statistics, level, identity)
    inverses = lax.all_gather(owned, "grad", axis=0, tiled=True)
    slots_here = grad_rows.shape[0]
    all_blocks = grad_rows.shape[1] // BLK
    pieces = grad_rows.astype(jnp.float32).reshape(slots_here, all_blocks, BLK)
    solved = jnp.einsum("rkj,kji->rki", pieces, inverses, precision=lax.Precision.HIGHEST)
    result = solved.reshape(slots_here, all_blocks * BLK)
    within = lax.axis_index("dp") * slots_here + lax.iota(jnp.int32, slots_here)
    live_mask = within < live_rows[0]
    return jnp.where(live_mask[:, None], result, jnp.zeros_like(result))


def solution(mesh):
    placed = (P("dp", "grad"), P(("grad", "dp"), None), P("grad"))
    return jax.shard_map(
        shards, mesh=mesh, in_specs=placed, out_specs=P(("grad", "dp"), None), check_vma=False
    )
```

profile of v0, /device:TPU:0, one launch (start us, length us, event | category | flops | bytes accessed | tf_op | source)
XLA Modules:
  0.0 596.3 jit_solution(16991862417378286354)
XLA Ops:
  6.5 1.3 copy.39
  8.2 11.6 %copy.41 = f32[8,160,160]{0,2,1:T(8,128)} copy(f32[8,160,160]{1,2,0:T(8,128)S(1)} %convolution_multiply_fusion) | data formatting | bytes 1638400 | tf_op jit(solution)/shard_map/mul | solution.py:26
  20.6 5.6 gather_fusion
  26.9 24.4 %psum.22 = f32[]{:T(128)} all-reduce(f32[]{:T(128)} %reduce_sum.9), channel_id=1, replica_groups=mesh['dp'=8,'grad'=4] {'dp'}, use_global_device_ids=true, to_apply=%region_2.3 | all-reduce | flops 1 | bytes 8 | tf_op jit(solution)/shard_map/psum | solution.py:29
  51.3 6.5 %psum.23 = f32[]{:T(128)} all-reduce(f32[]{:T(128)} %psum.22), channel_id=1, replica_groups=mesh['dp'=8,'grad'=4] {'grad'}, use_global_device_ids=true, to_apply=%region_3.4 | all-reduce | flops 1 | bytes 8 | tf_op jit(solution)/shard_map/psum | solution.py:30
  58.7 51.9 %all-reduce.5.cloned.1.call-done = f32[8,160,160]{1,2,0:T(8,128)} async-done(((f32[8,160,160]{1,2,0:T(8,128)}), f32[8,160,160]{1,2,0:T(8,128)}) %all-reduce.5.cloned.1.call-update) | async-done | bytes 819216 | tf_op jit(solution)/shard_map/psum | solution.py:29
  110.6 2.5 broadcast_add_fusion
  113.1 2.0 copy.42
  115.3 1.0 copy-done.2
  116.4 93.8 %custom-call.16 = f32[8,128,128]{2,1,0:T(8,128)S(1)} custom-call(f32[8,128,128]{2,1,0:T(8,128)S(1)} %cholesky.129), custom_call_target="Cholesky" | custom-call | tf_op jit(solution)/shard_map/jit(cholesky)/cholesky | solution.py:11
  210.4 78.6 %custom-call.17 = f32[8,1,128,128]{2,3,1,0:T(8,128)S(1)} custom-call(f32[8,1,128,128]{3,2,1,0:T(8,128)S(1)} %get-tuple-element.26), custom_call_target="InvertDiagBlocksLowerTriangular" | custom-call | tf_op jit(solution)/shard_map/jit(cholesky)/cholesky | solution.py:11
  289.0 1.5 constant_dynamic-update-slice_fusion.1
  290.5 1.2 convolution_subtract_fusion.1
  291.7 23.4 %custom-call.18 = f32[8,32,32]{2,1,0:T(8,128)S(1)} custom-call(f32[8,32,32]{2,1,0:T(8,128)S(1)} %convolution_subtract_fusion.1), custom_call_target="Cholesky" | custom-call | tf_op jit(solution)/shard_map/jit(cholesky)/cholesky | solution.py:11
  316.1 157.9 %custom-call.19 = f32[8,2,128,128]{2,3,1,0:T(8,128)} custom-call(f32[8,2,128,128]{3,2,1,0:T(8,128)S(1)} %pad_maximum_fusion), custom_call_target="InvertDiagBlocksLowerTriangular" | custom-call | tf_op jit(solution)/shard_map/triangular_solve | solution.py:12
  473.9 1.7 fusion.5
  475.7 1.3 convolution_subtract_fusion
  477.0 2.2 fusion.13
  479.2 2.5 fusion
  481.7 18.6 %copy.50 = bf16[1296,5120]{0,1:T(8,128)(2,1)} copy(bf16[1296,5120]{1,0:T(8,128)(2,1)} %param.4) | data formatting | bytes 26542080 | tf_op args[1]
  500.9 20.5 %all-gather.2.cloned.1.call-done = f32[32,160,160]{2,1,0:T(8,128)} async-done(((f32[8,160,160]{2,1,0:T(8,128)}), f32[32,160,160]{2,1,0:T(8,128)}) %all-gather.2.cloned.1.call-update) | async-done | bytes 3276816 | tf_op jit(solution)/shard_map/all_gather | solution.py:33
  521.5 21.6 %fusion.16 = f32[32,160,1296]{2,1,0:T(8,128)} fusion(f32[32,160,160]{2,1,0:T(8,128)} %all-gather.2.cloned.1.call-done, bf16[1296,32,160]{0,2,1:T(8,128)(2,1)} %bitcast.44), kind=kOutput, calls=%fused_computation.49 | convolution fusion | flops 12740198400 | bytes 43089920 | tf_op jit(solution)/shard_map/rkj,kji->rki/dot_general | solution.py:37
  543.1 27.9 %copy.52 = f32[1296,5120]{1,0:T(8,128)} copy(f32[1296,5120]{0,1:T(8,128)} %bitcast.43) | data formatting | bytes 53084160 | tf_op jit(solution)/shard_map/reshape | solution.py:38
  571.1 18.4 %broadcast_select_fusion = f32[1296,5120]{1,0:T(8,128)} fusion(f32[1296,5120]{1,0:T(8,128)} %copy.52, pred[1296]{0:T(1024)(128)(4,1)S(1)} %add_compare_fusion), kind=kLoop, calls=%fused_computation.1 | loop fusion | flops 6635520 | bytes 53085456 | tf_op jit(solution)/shard_map/jit(_where)/select_n | solution.py:41
  (37 shorter events, 3.2 us)
Async XLA Ops:
  8.2 11.6 %copy-start = (f32[8,160,160]{1,2,0:T(8,128)}, f32[8,160,160]{1,2,0:T(8,128)S(1)}, u32[]{:S(2)}) copy-start(f32[8,160,160]{1,2,0:T(8,128)S(1)} %convolution_multiply_fusion) | copy-start | bytes 2457604
  19.8 90.8 %all-reduce.5.cloned.1.call-start = ((), (), s32[]{:S(2)}) async-start(), calls=%async_computation | async-start | bytes 2621440 | tf_op jit(solution)/shard_map/psum | solution.py:29
  20.6 500.9 %all-gather.2.cloned.1.call-start = ((), (), s32[]{:S(2)}) async-start(), calls=%async_computation.1 | async-start | bytes 6553600 | tf_op jit(solution)/shard_map/all_gather | solution.py:33
  113.1 2.0 copy-start.1
  115.3 1.1 copy-start.2
Sparse Core Ops, SparseCore 0:
  24.2 86.3 all-reduce.4
  481.8 39.6 all-gather.1
where the time goes:
time: 598 us; the launch traced here: 596 us
  other arithmetic  376 us (63%)
  waiting for transfers between devices  73.2 us (12%)
  local copies, waits for them, and re-layouts  68.4 us (11%)
  matrix products  32.4 us (5%)
  blocking collectives  30.9 us (5%)
  between operations  15 us (3%)
    another operation x10, other arithmetic, invert_damped(): factors = jnp.linalg.cholesky(statistics + level * identity)  196 us
    another operation x7, other arithmetic, invert_damped(): lax.linalg.triangular_solve(factors, jnp.broadcast_to(identity, factors.s...  158 us
    psum x1, waiting for transfers between devices, shards(): statistics, column_trace = lax.psum((partial_value, diag_part), 'dp')  51.9 us
    reshape x1, local copies, waits for them, and re-layouts, shards(): result = solved.reshape(slots_here, all_blocks * BLK)  27.9 us
    psum x1, blocking collectives, shards(): statistics, column_trace = lax.psum((partial_value, diag_part), 'dp')  24.4 us
    dot_general x1, matrix products, shards(): jnp.einsum('rkj,kji->rki', pieces, inverses, precision=lax.Precision.HIGH...  21.6 us
    unnamed x8, local copies, waits for them, and re-layouts  20.9 us
    all_gather x1, waiting for transfers between devices, shards(): inverses = lax.all_gather(owned, 'grad', axis=0, tiled=True)  20.5 us
  transfers between devices with their start and end apart: 2, of which 2 were waited for; matrix products, arithmetic and copies ran while one was open for 4% of the time, Pallas kernels for 0%

commit v1 on v0

v1 whole, which is shorter than its diff:
```python
import functools

import jax
import jax.numpy as jnp
from jax import lax
from jax.experimental import pallas as pl
from jax.experimental.pallas import tpu as pltpu
from jax.sharding import PartitionSpec as P

D = 5120
BLK = 160
MAIN = 128
REST = BLK - MAIN
HALF = 64
ROWS = 104
GROUP = 4
WIDE = GROUP * BLK
TRACE_LANE = 72
VMEM = pl.BlockSpec(memory_space=pltpu.VMEM)
SMEM = pl.BlockSpec(memory_space=pltpu.SMEM)
HIGHEST = lax.Precision.HIGHEST


def iota(shape, dim):
    return lax.broadcasted_iota(jnp.int32, shape, dim)


def dot(a, b, ca, cb, precision=None):
    return lax.dot_general(
        a, b, (((ca,), (cb,)), ((), ())), precision=precision, preferred_element_type=jnp.float32
    )


def pack(b11, b21, b22, trace):
    top, low = b11[:HALF], pltpu.roll(b11[HALF:], HALF, 1)
    lane, row = iota((HALF, MAIN), 1), iota((HALF, MAIN), 0)
    first = jnp.where(lane < row, low, top)
    first = jnp.where(lane < HALF, first, top)
    diagonal = jnp.sum(jnp.where(lane == row, low, 0.0), axis=1, keepdims=True)
    wide = jnp.concatenate([b22, jnp.zeros((REST, MAIN - REST), jnp.float32)], axis=1)
    lane8, row8 = iota((8, MAIN), 1), iota((8, MAIN), 0)
    corner = wide[:8]
    for m in range(1, 4):
        corner = jnp.where(lane8 // REST == m, pltpu.roll(wide[8 * m : 8 * m + 8], REST * m, 1), corner)
    for g in range(8):
        corner = jnp.where(lane8 == HALF + g, diagonal[8 * g : 8 * g + 8], corner)
    corner = jnp.where(lane8 == TRACE_LANE, jnp.where(row8 == 0, trace, 0.0), corner)
    return first, b21, corner


def unpack(packed):
    first, b21, corner = packed[:HALF], packed[HALF : HALF + REST], packed[HALF + REST :]
    turned = first.T
    lane, row = iota((HALF, HALF), 1), iota((HALF, HALF), 0)
    a, at = first[:, :HALF], turned[:HALF]
    diagonal = jnp.concatenate([corner[:, HALF + g : HALF + g + 1] for g in range(8)], axis=0)
    p = jnp.where(lane >= row, a, at)
    r = jnp.where(lane < row, a, jnp.where(lane == row, diagonal, at))
    b11 = jnp.concatenate(
        [
            jnp.concatenate([p, first[:, HALF:]], axis=1),
            jnp.concatenate([turned[HALF:], r], axis=1),
        ],
        axis=0,
    )
    b22 = jnp.concatenate([corner[:, REST * m : REST * m + REST] for m in range(4)], axis=0)
    lane, row = iota((REST, REST), 1), iota((REST, REST), 0)
    b22 = jnp.where((row >= REST // 2) & (lane < REST // 2), b22.T, b22)
    return b11, b21, b22


def block_statistics(act_ref, index, scale):
    piece = act_ref[:, index * BLK : (index + 1) * BLK]
    return dot(piece, piece, 0, 0) * scale


def partial_trace(act_ref, scale):
    x = act_ref[...].astype(jnp.float32)
    return jnp.sum(x * x) * scale


def write(ref, at, parts):
    ref[at, 0:HALF] = parts[0]
    ref[at, HALF : HALF + REST] = parts[1]
    ref[at, HALF + REST : ROWS] = parts[2]


def pack_whole(s, trace):
    return pack(s[:MAIN, :MAIN], s[MAIN:, :MAIN], s[MAIN:, MAIN:], trace)


def statistics_kernel(scale, at_ref, act_ref, keep_ref, send_ref):
    z, y = at_ref[0], at_ref[1]
    trace = partial_trace(act_ref, scale)

    def emit(part, ref):
        for j in range(GROUP):
            s = block_statistics(act_ref, part * GROUP + j, scale)
            write(ref, jnp.bitwise_xor(z, j), pack_whole(s, trace))

    for mine in range(2):

        @pl.when(y == mine)
        def _():
            emit(mine, keep_ref)
            emit(1 - mine, send_ref)


def statistics_plain_kernel(scale, act_ref, out_ref):
    trace = partial_trace(act_ref, scale)
    for j in range(out_ref.shape[0]):
        write(out_ref, j, pack_whole(block_statistics(act_ref, j, scale), trace))


def eliminate(tiles, count):
    lane, sub = iota((8, MAIN), 1), iota((8, MAIN), 0)

    def spread(x):
        return jnp.broadcast_to(x, (8, MAIN))

    for r in range(count // 8):
        k = 8 * r
        t = tiles[r]
        inside = (lane >= k) & (lane < k + 8)
        rows = [
            jnp.where(inside, jnp.where(lane == k + i, 1.0, 0.0), spread(t[i : i + 1, :]))
            for i in range(8)
        ]
        small = [[spread(t[i : i + 1, k + j : k + j + 1]) for j in range(8)] for i in range(8)]
        for a in range(8):
            pivot = 1.0 / small[a][a]
            rows[a] = rows[a] * pivot
            for b in range(a + 1, 8):
                small[a][b] = small[a][b] * pivot
            for c in range(8):
                if c != a:
                    factor = small[c][a]
                    rows[c] = rows[c] - factor * rows[a]
                    for b in range(a + 1, 8):
                        small[c][b] = small[c][b] - factor * small[a][b]
        rows = [jnp.where(inside, -x, x) for x in rows]
        for j in range(len(tiles)):
            total = None
            for i in range(8):
                if j == r:
                    column = jnp.where(sub == i, -1.0, 0.0)
                else:
                    column = spread(tiles[j][:, k + i : k + i + 1])
                total = column * rows[i] if total is None else total + column * rows[i]
            tiles[j] = -total if j == r else jnp.where(inside, 0.0, tiles[j]) - total
    return tiles


def invert(packed, level):
    b11, b21, b22 = unpack(packed)
    lane, row = iota((MAIN, MAIN), 1), iota((MAIN, MAIN), 0)
    b11 = jnp.where(lane == row, b11 + level, b11)
    tiles = [b11[8 * r : 8 * r + 8] for r in range(MAIN // 8)]
    tiles += [b21[8 * r : 8 * r + 8] for r in range(REST // 8)]
    tiles = eliminate(tiles, MAIN)
    inner = jnp.concatenate(tiles[: MAIN // 8], axis=0)
    ratio = jnp.concatenate(tiles[MAIN // 8 :], axis=0)
    lane, row = iota((REST, REST), 1), iota((REST, REST), 0)
    schur = jnp.where(lane == row, b22 + level, b22) - dot(ratio, b21, 1, 1, HIGHEST)
    schur = jnp.concatenate([schur, jnp.zeros((REST, MAIN - REST), jnp.float32)], axis=1)
    last = eliminate([schur[8 * r : 8 * r + 8] for r in range(REST // 8)], REST)
    last = -jnp.concatenate(last, axis=0)[:, :REST]
    side = dot(last, ratio, 1, 0, HIGHEST)
    return pack(dot(ratio, side, 0, 0, HIGHEST) - inner, -side, last, 0.0)


def damping(total):
    return 0.5 * total / D + 1e-06


def invert_kernel(own_ref, a_ref, b_ref, out_ref):
    trace = a_ref[0:1, TRACE_LANE : TRACE_LANE + 1] + b_ref[0:1, TRACE_LANE : TRACE_LANE + 1]
    write(out_ref, 0, invert(own_ref[...], damping(trace)))


def invert_plain_kernel(total_ref, in_ref, out_ref):
    write(out_ref, 0, invert(in_ref[0], damping(total_ref[0])))


def build_weights(packed_ref, first, z, top_ref, mid_ref, end_ref):
    top_ref[...] = jnp.zeros_like(top_ref)
    mid_ref[...] = jnp.zeros_like(mid_ref)
    end_ref[...] = jnp.zeros_like(end_ref)
    for s in range(GROUP):
        b11, b21, b22 = unpack(packed_ref[first + jnp.bitwise_xor(z, s)])
        whole = jnp.concatenate(
            [jnp.concatenate([b11, b21.T], axis=1), jnp.concatenate([b21, b22], axis=1)], axis=0
        )
        high = whole.astype(jnp.bfloat16)
        low = (whole - high.astype(jnp.float32)).astype(jnp.bfloat16)
        lo = s * BLK
        if s < 2:
            cut = min(256 - lo, BLK)
            top_ref[lo : lo + BLK, lo : lo + cut] = high[:, :cut]
            top_ref[384 + lo : 384 + lo + BLK, lo : lo + cut] = low[:, :cut]
        if s == 1:
            mid_ref[lo - 128 : lo - 128 + BLK, 0 : lo + BLK - 256] = high[:, 256 - lo :]
            mid_ref[384 + lo : 384 + lo + BLK, 0 : lo + BLK - 256] = low[:, 256 - lo :]
        if s == 2:
            mid_ref[lo - 128 : lo - 128 + BLK, lo - 256 : lo - 256 + BLK] = high
            mid_ref[384 + lo : 384 + lo + BLK, lo - 256 : lo - 256 + BLK] = low
        if s == 3:
            mid_ref[lo - 128 : lo - 128 + BLK, lo - 256 : 256] = high[:, :32]
            mid_ref[384 + lo : 384 + lo + BLK, lo - 256 : 256] = low[:, :32]
            end_ref[lo - 384 : lo - 384 + BLK, 0:128] = high[:, 32:]
            end_ref[lo - 384 : lo - 384 + BLK, 128:256] = low[:, 32:]


def apply_kernel(n_groups, at_ref, *refs):
    packed = refs[:n_groups]
    grad_ref = refs[n_groups]
    out_ref, top_ref, mid_ref, end_ref = refs[-4:]
    z, live, start = at_ref[0], at_ref[1], at_ref[2]
    which, tile = pl.program_id(0), pl.program_id(1)
    for g in range(n_groups):

        @pl.when((tile == 0) & (which == g))
        def _():
            build_weights(packed[g], 0, z, top_ref, mid_ref, end_ref)

    x = grad_ref[...]
    left, right = x[:, :384], x[:, 128:]
    rows = x.shape[0]
    within = start + tile * rows + iota((rows, 1), 0)
    keep = within < live
    a = dot(jnp.concatenate([left, left], axis=1), top_ref[...], 1, 0)
    out_ref[:, 0:256] = jnp.where(keep, a, 0.0)
    b = dot(jnp.concatenate([right, right], axis=1), mid_ref[...], 1, 0)
    out_ref[:, 256:512] = jnp.where(keep, b, 0.0)
    c = dot(x[:, 384:], end_ref[...], 1, 0)
    out_ref[:, 512:640] = jnp.where(keep, c[:, :128] + c[:, 128:], 0.0)


def row_tile(rows):
    for parts in range(1, rows + 1):
        if rows % parts == 0 and rows // parts <= 432 and (rows // parts) % 16 == 0:
            return rows // parts
    return rows


def apply(groups, columns, grad_rows, z, live, start, before):
    rows = grad_rows.shape[0]
    tile = row_tile(rows)
    n = len(groups)
    at = jnp.stack([z, live, start, *columns]).astype(jnp.int32)

    def column(g, t, at_ref):
        return (t, at_ref[3 + g])

    spec = pl.BlockSpec((tile, WIDE), column)
    ins = [pl.BlockSpec((GROUP, ROWS, MAIN), lambda g, t, at_ref: (0, 0, 0))] * n + [spec]
    args = [*groups, grad_rows]
    aliases = {}
    if before is not None:
        ins.append(pl.BlockSpec(memory_space=pl.ANY))
        args.append(before)
        aliases = {1 + n + 1: 0}
    return pl.pallas_call(
        functools.partial(apply_kernel, n),
        out_shape=jax.ShapeDtypeStruct((rows, D), jnp.float32),
        grid_spec=pltpu.PrefetchScalarGridSpec(
            num_scalar_prefetch=1,
            grid=(n, rows // tile),
            in_specs=ins,
            out_specs=spec,
            scratch_shapes=[
                pltpu.VMEM((768, 256), jnp.bfloat16),
                pltpu.VMEM((1024, 256), jnp.bfloat16),
                pltpu.VMEM((256, 256), jnp.bfloat16),
            ],
        ),
        input_output_aliases=aliases,
        cost_estimate=pl.CostEstimate(
            flops=4 * rows * WIDE * 256 * n, bytes_accessed=6 * rows * WIDE * n, transcendentals=0
        ),
        name="apply",
    )(at, *args)


def swap(x, axis, mask):
    size = lax.axis_size(axis)
    return lax.ppermute(x, axis, [(i, i ^ mask) for i in range(size)])


def shards_small(activations, grad_rows, live_rows):
    scale = 1.0 / (activations.shape[0] * lax.axis_size("dp"))
    i, g = lax.axis_index("dp"), lax.axis_index("grad")
    z, y = i // 2, i % 2
    four = jax.ShapeDtypeStruct((GROUP, ROWS, MAIN), jnp.float32)
    keep, send = pl.pallas_call(
        functools.partial(statistics_kernel, scale),
        out_shape=(four, four),
        in_specs=[SMEM, VMEM],
        out_specs=(VMEM, VMEM),
        name="statistics",
    )(jnp.stack([z, y]).astype(jnp.int32), activations)
    half = keep + swap(send, "dp", 1)
    own = half[0] + swap(half[1], "dp", 2) + swap(half[2], "dp", 4) + swap(half[3], "dp", 6)
    mark = own[HALF + REST :]
    mark = mark + swap(mark, "grad", 2)
    inverse = pl.pallas_call(
        invert_kernel,
        out_shape=jax.ShapeDtypeStruct((1, ROWS, MAIN), jnp.float32),
        in_specs=[VMEM] * 3,
        out_specs=VMEM,
        name="invert",
    )(own, mark, swap(mark, "grad", 1))
    mine = jnp.concatenate([inverse] + [swap(inverse, "dp", d) for d in (2, 4, 6)], axis=0)
    by_y, by_x, by_core = swap(mine, "dp", 1), swap(mine, "grad", 2), swap(mine, "grad", 1)
    by_xy = swap(by_y, "grad", 2)
    by_y_core, by_x_core = swap(by_y, "grad", 1), swap(by_x, "grad", 1)
    by_xy_core = swap(by_xy, "grad", 1)
    live = live_rows[0]
    start = i * grad_rows.shape[0]

    def column(dg, dy):
        return (g ^ dg) * 2 + (y ^ dy)

    out = apply([mine, by_core], [column(0, 0), column(1, 0)], grad_rows, z, live, start, None)
    out = apply(
        [by_y, by_x, by_y_core, by_x_core],
        [column(0, 1), column(2, 0), column(1, 1), column(3, 0)],
        grad_rows, z, live, start, out,
    )
    return apply([by_xy, by_xy_core], [column(2, 1), column(3, 1)], grad_rows, z, live, start, out)


def shards_any(activations, grad_rows, live_rows):
    scale = 1.0 / (activations.shape[0] * lax.axis_size("dp"))
    col_blocks = activations.shape[1] // BLK
    part = pl.pallas_call(
        functools.partial(statistics_plain_kernel, scale),
        out_shape=jax.ShapeDtypeStruct((col_blocks, ROWS, MAIN), jnp.float32),
        in_specs=[VMEM],
        out_specs=VMEM,
        name="statistics",
    )(activations)
    packed = lax.psum(part, "dp")
    total = lax.psum(packed[0, HALF + REST, TRACE_LANE].reshape(1), "grad")
    block = pl.BlockSpec((1, ROWS, MAIN), lambda b: (b, 0, 0))
    owned = pl.pallas_call(
        invert_plain_kernel,
        out_shape=jax.ShapeDtypeStruct((col_blocks, ROWS, MAIN), jnp.float32),
        grid=(col_blocks,),
        in_specs=[SMEM, block],
        out_specs=block,
        name="invert",
    )(total, packed)
    inverses = lax.all_gather(owned, "grad", axis=0, tiled=True)
    n = D // WIDE
    groups = [inverses[GROUP * j : GROUP * j + GROUP] for j in range(n)]
    start = lax.axis_index("dp") * grad_rows.shape[0]
    return apply(
        groups, [jnp.int32(j) for j in range(n)], grad_rows, jnp.int32(0), live_rows[0], start, None
    )


def solution(mesh):
    placed = (P("dp", "grad"), P(("grad", "dp"), None), P("grad"))
    small = mesh.shape["dp"] == 8 and mesh.shape["grad"] == 4
    return jax.shard_map(
        shards_small if small else shards_any,
        mesh=mesh, in_specs=placed, out_specs=P(("grad", "dp"), None), check_vma=False,
    )
```

time: 598 us -> 104 us (0.17)
  other arithmetic: 376 us -> 2.43 us
  local copies, waits for them, and re-layouts: 68.4 us -> 5.17 us
  Pallas kernels: 0 us -> 53.8 us
  waiting for transfers between devices: 73.2 us -> 22.2 us
  matrix products: 32.4 us -> 0 us
  blocking collectives: 30.9 us -> 0 us
  starting transfers between devices: 0.04 us -> 18.5 us
  between operations: 15 us -> 0.75 us
    another operation x17 -> x1, other arithmetic: 355 us -> 0.61 us  [shards_small(): jnp.stack([z, y]).astype(jnp.int32)]
    pallas_call x0 -> x5, Pallas kernels: none -> 53.8 us  [the longest x3 40.2 us: apply(): pl.pallas_call(functools.partial(apply_kernel, n), out_shape=jax.ShapeDty...]
    psum x1 -> x0, waiting for transfers between devices: 51.9 us -> none  [shards(): statistics, column_trace = lax.psum((partial_value, diag_part), 'dp')]
    psum x2 -> x0, blocking collectives: 30.9 us -> none  [the longest x1 24.4 us: shards(): statistics, column_trace = lax.psum((partial_value, diag_part), 'dp')]
    reshape x1 -> x0, local copies, waits for them, and re-layouts: 27.9 us -> none  [shards(): result = solved.reshape(slots_here, all_blocks * BLK)]
    dot_general x3 -> x0, matrix products: 24.5 us -> none  [the longest x1 21.6 us: shards(): jnp.einsum('rkj,kji->rki', pieces, inverses, precision=lax.Precision.HIGH...]
    ppermute x0 -> x16, waiting for transfers between devices: none -> 22.2 us  [swap(): return lax.ppermute(x, axis, [(i, i ^ mask) for i in range(size)])]
    all_gather x1 -> x0, waiting for transfers between devices: 20.5 us -> none  [shards(): inverses = lax.all_gather(owned, 'grad', axis=0, tiled=True)]
  transfers between devices with their start and end apart: 2 -> 16, of which waited for: 2 -> 10; matrix products, arithmetic and copies ran while one was open for 4% -> 2% of each run, Pallas kernels for 0% -> 29%
where the time goes in v1:
time: 104 us; the launch traced here: 103 us
  Pallas kernels  53.8 us (52%)
  waiting for transfers between devices  22.2 us (21%)
  starting transfers between devices  18.5 us (18%)
  local copies, waits for them, and re-layouts  5.17 us (5%)
  other arithmetic  2.43 us (2%)
    pallas_call x3, Pallas kernels, apply(): pl.pallas_call(functools.partial(apply_kernel, n), out_shape=jax.ShapeDty...  40.2 us
    ppermute x16, waiting for transfers between devices, swap(): return lax.ppermute(x, axis, [(i, i ^ mask) for i in range(size)])  22.2 us
    ppermute x16, starting transfers between devices, swap(): return lax.ppermute(x, axis, [(i, i ^ mask) for i in range(size)])  18.5 us
    pallas_call x1, Pallas kernels, shards_small(): pl.pallas_call(invert_kernel, out_shape=jax.ShapeDtypeStruct((1, ROWS, MA...  9.13 us
    pallas_call x1, Pallas kernels, shards_small(): pl.pallas_call(functools.partial(statistics_kernel, scale), out_shape=(fo...  4.43 us
    unnamed x22, local copies, waits for them, and re-layouts  3.34 us
  transfers between devices with their start and end apart: 16, of which 10 were waited for; matrix products, arithmetic and copies ran while one was open for 2% of the time, Pallas kernels for 29%

profile of v1, /device:TPU:0, one launch (start us, length us, event | category | flops | bytes accessed | tf_op | source)
XLA Modules:
  0.0 102.9 jit_solution(2214893524552153051)
XLA Ops:
  0.6 4.4 %statistics.1 = (f32[4,104,128]{2,1,0:T(8,128)}, f32[4,104,128]{2,1,0:T(8,128)}) custom-call(s32[2]{0:T(128)} %pad_add_fusion.at_ref, bf16[256,1280]{1,0:T(8,128)(2,1)} %act_ref.1), custom_call_target="tpu_custom_call" | custom-call | tf_op jit(solution)/shard_map/statistics/pallas_call | solution.py:295
  5.0 3.0 %collective-permute-start = (f32[4,104,128]{2,1,0:T(8,128)}, f32[4,104,128]{2,1,0:T(8,128)S(1)}, u32[]{:S(2)}, u32[]{:S(2)}) collective-permute-start(f32[4,104,128]{2,1,0:T(8,128)} %get-tuple-element.8), channel_id=1, source_target_pairs={{0,4},{4,0},{8,12},{12,8},{16,20},{20,16},{24,28},{28,24},{1,5},{5... | collective-permute-start | bytes 638984 | tf_op jit(solution)/shard_map/ppermute | solution.py:287
  8.0 5.5 %collective-permute-done = f32[4,104,128]{2,1,0:T(8,128)S(1)} collective-permute-done((f32[4,104,128]{2,1,0:T(8,128)}, f32[4,104,128]{2,1,0:T(8,128)S(1)}, u32[]{:S(2)}, u32[]{:S(2)}) %collective-permute-start) | collective-permute-done | bytes 213024 | tf_op jit(solution)/shard_map/ppermute | solution.py:287
  13.5 1.0 add.47
  14.5 1.9 %collective-permute-start.1 = (f32[104,128]{1,0:T(8,128)S(1)}, f32[104,128]{1,0:T(8,128)S(1)}, u32[]{:S(2)}, u32[]{:S(2)}) collective-permute-start(f32[104,128]{1,0:T(8,128)S(1)} %get-tuple-element.9), channel_id=1, source_target_pairs={{0,8},{4,12},{8,0},{12,4},{16,24},{20,28},{24,16},{28,20},{1,9},{5... | collective-permute-start | bytes 159752 | tf_op jit(solution)/shard_map/ppermute | solution.py:287
  16.3 2.6 %collective-permute-start.2 = (f32[104,128]{1,0:T(8,128)S(1)}, f32[104,128]{1,0:T(8,128)S(1)}, u32[]{:S(2)}, u32[]{:S(2)}) collective-permute-start(f32[104,128]{1,0:T(8,128)S(1)} %get-tuple-element.11), channel_id=1, source_target_pairs={{0,16},{4,20},{8,24},{12,28},{16,0},{20,4},{24,8},{28,12},{1,17},{... | collective-permute-start | bytes 159752 | tf_op jit(solution)/shard_map/ppermute | solution.py:287
  19.1 3.4 %collective-permute-done.2 = f32[104,128]{1,0:T(8,128)S(1)} collective-permute-done((f32[104,128]{1,0:T(8,128)S(1)}, f32[104,128]{1,0:T(8,128)S(1)}, u32[]{:S(2)}, u32[]{:S(2)}) %collective-permute-start.2) | collective-permute-done | bytes 53280 | tf_op jit(solution)/shard_map/ppermute | solution.py:287
  22.5 2.3 %collective-permute-done.3 = f32[104,128]{1,0:T(8,128)S(1)} collective-permute-done((f32[104,128]{1,0:T(8,128)S(1)}, f32[104,128]{1,0:T(8,128)S(1)}, u32[]{:S(2)}, u32[]{:S(2)}) %collective-permute-start.3) | collective-permute-done | bytes 53280 | tf_op jit(solution)/shard_map/ppermute | solution.py:287
  24.9 1.6 %collective-permute-start.4 = (f32[8,128]{1,0:T(8,128)S(1)}, f32[8,128]{1,0:T(8,128)S(1)}, u32[]{:S(2)}, u32[]{:S(2)}) collective-permute-start(f32[8,128]{1,0:T(8,128)S(1)} %slice.24), channel_id=1, source_target_pairs={{0,2},{1,3},{2,0},{3,1},{4,6},{5,7},{6,4},{7,5},{8,10},{9,11},{10,... | collective-permute-start | bytes 12296 | tf_op jit(solution)/shard_map/ppermute | solution.py:287
  26.4 2.1 %collective-permute-done.4 = f32[8,128]{1,0:T(8,128)S(1)} collective-permute-done((f32[8,128]{1,0:T(8,128)S(1)}, f32[8,128]{1,0:T(8,128)S(1)}, u32[]{:S(2)}, u32[]{:S(2)}) %collective-permute-start.4) | collective-permute-done | bytes 4128 | tf_op jit(solution)/shard_map/ppermute | solution.py:287
  28.6 1.2 %collective-permute-done.5.b_ref = f32[8,128]{1,0:T(8,128)S(1)} collective-permute-done((f32[8,128]{1,0:T(8,128)S(1)}, f32[8,128]{1,0:T(8,128)S(1)}, u32[]{:S(2)}, u32[]{:S(2)}) %collective-permute-start.5) | collective-permute-done | bytes 4128 | tf_op jit(solution)/shard_map/ppermute | solution.py:287
  30.3 9.1 %invert.1 = f32[1,104,128]{2,1,0:T(8,128)} custom-call(f32[104,128]{1,0:T(8,128)} %copy-done.1, f32[8,128]{1,0:T(8,128)} %copy-done.9, f32[8,128]{1,0:T(8,128)} %copy-done.10), custom_call_target="tpu_custom_call" | custom-call | tf_op jit(solution)/shard_map/invert/pallas_call | solution.py:306
  39.5 1.2 %collective-permute-start.7 = (f32[1,104,128]{2,1,0:T(8,128)}, f32[1,104,128]{2,1,0:T(8,128)S(1)}, u32[]{:S(2)}, u32[]{:S(2)}) collective-permute-start(f32[1,104,128]{2,1,0:T(8,128)} %invert.1), channel_id=1, source_target_pairs={{0,16},{4,20},{8,24},{12,28},{16,0},{20,4},{24,8},{28,12},{1,17},{... | collective-permute-start | bytes 159752 | tf_op jit(solution)/shard_map/ppermute | solution.py:287
  40.7 3.1 %collective-permute-start.8 = (f32[1,104,128]{2,1,0:T(8,128)}, f32[1,104,128]{2,1,0:T(8,128)S(1)}, u32[]{:S(2)}, u32[]{:S(2)}) collective-permute-start(f32[1,104,128]{2,1,0:T(8,128)} %invert.1), channel_id=1, source_target_pairs={{0,24},{4,28},{8,16},{12,20},{16,8},{20,12},{24,0},{28,4},{1,25},{... | collective-permute-start | bytes 159752 | tf_op jit(solution)/shard_map/ppermute | solution.py:287
  44.6 2.7 %collective-permute-done.7 = f32[1,104,128]{2,1,0:T(8,128)S(1)} collective-permute-done((f32[1,104,128]{2,1,0:T(8,128)}, f32[1,104,128]{2,1,0:T(8,128)S(1)}, u32[]{:S(2)}, u32[]{:S(2)}) %collective-permute-start.7) | collective-permute-done | bytes 53280 | tf_op jit(solution)/shard_map/ppermute | solution.py:287
  47.3 0.8 pad_maximum_fusion.refs_0_
  48.2 1.6 %collective-permute-start.9 = (f32[4,104,128]{2,1,0:T(8,128)S(1)}, f32[4,104,128]{2,1,0:T(8,128)S(1)}, u32[]{:S(2)}, u32[]{:S(2)}) collective-permute-start(f32[4,104,128]{2,1,0:T(8,128)S(1)} %pad_maximum_fusion.refs_0_), channel_id=1, source_target_pairs={{0,4},{4,0},{8,12},{12,8},{16,20},{20,16},{24,28},{28,24},{1,5},{5... | collective-permute-start | bytes 638984 | tf_op jit(solution)/shard_map/ppermute | solution.py:287
  49.8 1.5 %collective-permute-start.12 = (f32[4,104,128]{2,1,0:T(8,128)S(1)}, f32[4,104,128]{2,1,0:T(8,128)S(1)}, u32[]{:S(2)}, u32[]{:S(2)}) collective-permute-start(f32[4,104,128]{2,1,0:T(8,128)S(1)} %pad_maximum_fusion.refs_0_), channel_id=1, source_target_pairs={{0,2},{1,3},{2,0},{3,1},{4,6},{5,7},{6,4},{7,5},{8,10},{9,11},{10,... | collective-permute-start | bytes 638984 | tf_op jit(solution)/shard_map/ppermute | solution.py:287
  51.3 2.8 %collective-permute-done.9.refs_0_ = f32[4,104,128]{2,1,0:T(8,128)S(1)} collective-permute-done((f32[4,104,128]{2,1,0:T(8,128)S(1)}, f32[4,104,128]{2,1,0:T(8,128)S(1)}, u32[]{:S(2)}, u32[]{:S(2)}) %collective-permute-start.9) | collective-permute-done | bytes 213024 | tf_op jit(solution)/shard_map/ppermute | solution.py:287
  54.1 1.5 %collective-permute-start.10 = (f32[4,104,128]{2,1,0:T(8,128)S(1)}, f32[4,104,128]{2,1,0:T(8,128)S(1)}, u32[]{:S(2)}, u32[]{:S(2)}) collective-permute-start(f32[4,104,128]{2,1,0:T(8,128)S(1)} %collective-permute-done.9.refs_0_), channel_id=1, source_target_pairs={{0,2},{1,3},{2,0},{3,1},{4,6},{5,7},{6,4},{7,5},{8,10},{9,11},{10,... | collective-permute-start | bytes 638984 | tf_op jit(solution)/shard_map/ppermute | solution.py:287
  55.6 1.3 %collective-permute-done.12.refs_1_ = f32[4,104,128]{2,1,0:T(8,128)S(1)} collective-permute-done((f32[4,104,128]{2,1,0:T(8,128)S(1)}, f32[4,104,128]{2,1,0:T(8,128)S(1)}, u32[]{:S(2)}, u32[]{:S(2)}) %collective-permute-start.12) | collective-permute-done | bytes 213024 | tf_op jit(solution)/shard_map/ppermute | solution.py:287
  60.0 10.8 %apply.3.refs_5_ = f32[1296,5120]{1,0:T(8,128)} custom-call(s32[5]{0:T(128)} %stack.64.at_ref, f32[4,104,128]{2,1,0:T(8,128)} %copy-done, f32[4,104,128]{2,1,0:T(8,128)} %copy-done.7, bf16[1296,5120]{1,0:T(8,128)(2,1)} %refs_2_.3), custom_call_target="tpu_custom_call" | custom-call | flops 1698693120 | bytes 9953280 | tf_op jit(solution)/shard_map/apply/pallas_call | solution.py:263
  72.8 18.7 %apply.4.refs_3_ = f32[1296,5120]{1,0:T(8,128)} custom-call(s32[7]{0:T(128)} %stack.61.at_ref, f32[4,104,128]{2,1,0:T(8,128)} %copy-done.2, f32[4,104,128]{2,1,0:T(8,128)} %copy-done.3, f32[4,104,128]{2,1,0:T(8,128)} %copy-done.5, f32[4,104,128]{2,1,0:T(8,128)} %copy-done.6, bf16[1296,5120]{1,0:T(8,128)(2,1)} %refs_2_.3, ...), custom_call_target="tpu_custom_call", output_to_operand_aliasing={{}: (6, {})} | custom-call | flops 3397386240 | bytes 19906560 | tf_op jit(solution)/shard_map/apply/pallas_call | solution.py:263
  92.2 10.6 %apply.5 = f32[1296,5120]{1,0:T(8,128)} custom-call(s32[5]{0:T(128)} %stack.54.at_ref, f32[4,104,128]{2,1,0:T(8,128)} %copy-done.4, f32[4,104,128]{2,1,0:T(8,128)} %copy-done.8, bf16[1296,5120]{1,0:T(8,128)(2,1)} %refs_2_.3, f32[1296,5120]{1,0:T(8,128)} %apply.4.refs_3_), custom_call_target="tpu_custom_call", output_to_operand_aliasing={{}: (4, {})} | custom-call | flops 1698693120 | bytes 9953280 | tf_op jit(solution)/shard_map/apply/pallas_call | solution.py:263
  (45 shorter events, 7.4 us)
Async XLA Ops:
  5.0 8.4 %collective-permute-start = (f32[4,104,128]{2,1,0:T(8,128)}, f32[4,104,128]{2,1,0:T(8,128)S(1)}, u32[]{:S(2)}, u32[]{:S(2)}) collective-permute-start(f32[4,104,128]{2,1,0:T(8,128)} %get-tuple-element.8), channel_id=1, source_target_pairs={{0,4},{4,0},{8,12},{12,8},{16,20},{20,16},{24,28},{28,24},{1,5},{5... | collective-permute-start | bytes 638984 | tf_op jit(solution)/shard_map/ppermute | solution.py:287
  14.5 4.7 %collective-permute-start.1 = (f32[104,128]{1,0:T(8,128)S(1)}, f32[104,128]{1,0:T(8,128)S(1)}, u32[]{:S(2)}, u32[]{:S(2)}) collective-permute-start(f32[104,128]{1,0:T(8,128)S(1)} %get-tuple-element.9), channel_id=1, source_target_pairs={{0,8},{4,12},{8,0},{12,4},{16,24},{20,28},{24,16},{28,20},{1,9},{5... | collective-permute-start | bytes 159752 | tf_op jit(solution)/shard_map/ppermute | solution.py:287
  16.3 6.2 %collective-permute-start.2 = (f32[104,128]{1,0:T(8,128)S(1)}, f32[104,128]{1,0:T(8,128)S(1)}, u32[]{:S(2)}, u32[]{:S(2)}) collective-permute-start(f32[104,128]{1,0:T(8,128)S(1)} %get-tuple-element.11), channel_id=1, source_target_pairs={{0,16},{4,20},{8,24},{12,28},{16,0},{20,4},{24,8},{28,12},{1,17},{... | collective-permute-start | bytes 159752 | tf_op jit(solution)/shard_map/ppermute | solution.py:287
  18.9 5.9 %collective-permute-start.3 = (f32[104,128]{1,0:T(8,128)S(1)}, f32[104,128]{1,0:T(8,128)S(1)}, u32[]{:S(2)}, u32[]{:S(2)}) collective-permute-start(f32[104,128]{1,0:T(8,128)S(1)} %get-tuple-element.10), channel_id=1, source_target_pairs={{0,24},{4,28},{8,16},{12,20},{16,8},{20,12},{24,0},{28,4},{1,25},{... | collective-permute-start | bytes 159752 | tf_op jit(solution)/shard_map/ppermute | solution.py:287
  24.9 4.9 %copy-start.1 = (f32[104,128]{1,0:T(8,128)}, f32[104,128]{1,0:T(8,128)S(1)}, u32[]{:S(2)}) copy-start(f32[104,128]{1,0:T(8,128)S(1)} %fusion.2.own_ref) | copy-start | bytes 159748
  24.9 3.7 %collective-permute-start.4 = (f32[8,128]{1,0:T(8,128)S(1)}, f32[8,128]{1,0:T(8,128)S(1)}, u32[]{:S(2)}, u32[]{:S(2)}) collective-permute-start(f32[8,128]{1,0:T(8,128)S(1)} %slice.24), channel_id=1, source_target_pairs={{0,2},{1,3},{2,0},{3,1},{4,6},{5,7},{6,4},{7,5},{8,10},{9,11},{10,... | collective-permute-start | bytes 12296 | tf_op jit(solution)/shard_map/ppermute | solution.py:287
  28.6 1.2 %copy-start.9 = (f32[8,128]{1,0:T(8,128)}, f32[8,128]{1,0:T(8,128)S(1)}, u32[]{:S(2)}) copy-start(f32[8,128]{1,0:T(8,128)S(1)} %slice_add_fusion.a_ref) | copy-start | bytes 12292
  28.6 1.2 %collective-permute-start.5 = (f32[8,128]{1,0:T(8,128)S(1)}, f32[8,128]{1,0:T(8,128)S(1)}, u32[]{:S(2)}, u32[]{:S(2)}) collective-permute-start(f32[8,128]{1,0:T(8,128)S(1)} %slice_add_fusion.a_ref), channel_id=1, source_target_pairs={{0,1},{1,0},{2,3},{3,2},{4,5},{5,4},{6,7},{7,6},{8,9},{9,8},{10,11... | collective-permute-start | bytes 12296 | tf_op jit(solution)/shard_map/ppermute | solution.py:287
  39.5 5.2 %collective-permute-start.6 = (f32[1,104,128]{2,1,0:T(8,128)}, f32[1,104,128]{2,1,0:T(8,128)S(1)}, u32[]{:S(2)}, u32[]{:S(2)}) collective-permute-start(f32[1,104,128]{2,1,0:T(8,128)} %invert.1), channel_id=1, source_target_pairs={{0,8},{4,12},{8,0},{12,4},{16,24},{20,28},{24,16},{28,20},{1,9},{5... | collective-permute-start | bytes 159752 | tf_op jit(solution)/shard_map/ppermute | solution.py:287
  39.5 7.9 %collective-permute-start.7 = (f32[1,104,128]{2,1,0:T(8,128)}, f32[1,104,128]{2,1,0:T(8,128)S(1)}, u32[]{:S(2)}, u32[]{:S(2)}) collective-permute-start(f32[1,104,128]{2,1,0:T(8,128)} %invert.1), channel_id=1, source_target_pairs={{0,16},{4,20},{8,24},{12,28},{16,0},{20,4},{24,8},{28,12},{1,17},{... | collective-permute-start | bytes 159752 | tf_op jit(solution)/shard_map/ppermute | solution.py:287
  40.7 6.6 %collective-permute-start.8 = (f32[1,104,128]{2,1,0:T(8,128)}, f32[1,104,128]{2,1,0:T(8,128)S(1)}, u32[]{:S(2)}, u32[]{:S(2)}) collective-permute-start(f32[1,104,128]{2,1,0:T(8,128)} %invert.1), channel_id=1, source_target_pairs={{0,24},{4,28},{8,16},{12,20},{16,8},{20,12},{24,0},{28,4},{1,25},{... | collective-permute-start | bytes 159752 | tf_op jit(solution)/shard_map/ppermute | solution.py:287
  48.2 11.2 %copy-start = (f32[4,104,128]{2,1,0:T(8,128)}, f32[4,104,128]{2,1,0:T(8,128)S(1)}, u32[]{:S(2)}) copy-start(f32[4,104,128]{2,1,0:T(8,128)S(1)} %pad_maximum_fusion.refs_0_) | copy-start | bytes 638980
  48.2 5.9 %collective-permute-start.9 = (f32[4,104,128]{2,1,0:T(8,128)S(1)}, f32[4,104,128]{2,1,0:T(8,128)S(1)}, u32[]{:S(2)}, u32[]{:S(2)}) collective-permute-start(f32[4,104,128]{2,1,0:T(8,128)S(1)} %pad_maximum_fusion.refs_0_), channel_id=1, source_target_pairs={{0,4},{4,0},{8,12},{12,8},{16,20},{20,16},{24,28},{28,24},{1,5},{5... | collective-permute-start | bytes 638984 | tf_op jit(solution)/shard_map/ppermute | solution.py:287
  49.8 7.1 %collective-permute-start.12 = (f32[4,104,128]{2,1,0:T(8,128)S(1)}, f32[4,104,128]{2,1,0:T(8,128)S(1)}, u32[]{:S(2)}, u32[]{:S(2)}) collective-permute-start(f32[4,104,128]{2,1,0:T(8,128)S(1)} %pad_maximum_fusion.refs_0_), channel_id=1, source_target_pairs={{0,2},{1,3},{2,0},{3,1},{4,6},{5,7},{6,4},{7,5},{8,10},{9,11},{10,... | collective-permute-start | bytes 638984 | tf_op jit(solution)/shard_map/ppermute | solution.py:287
  51.3 8.1 %collective-permute-start.15 = (f32[4,104,128]{2,1,0:T(8,128)S(1)}, f32[4,104,128]{2,1,0:T(8,128)S(1)}, u32[]{:S(2)}, u32[]{:S(2)}) collective-permute-start(f32[4,104,128]{2,1,0:T(8,128)S(1)} %pad_maximum_fusion.refs_0_), channel_id=1, source_target_pairs={{0,1},{1,0},{2,3},{3,2},{4,5},{5,4},{6,7},{7,6},{8,9},{9,8},{10,11... | collective-permute-start | bytes 638984 | tf_op jit(solution)/shard_map/ppermute | solution.py:287
  54.1 17.3 %copy-start.2 = (f32[4,104,128]{2,1,0:T(8,128)}, f32[4,104,128]{2,1,0:T(8,128)S(1)}, u32[]{:S(2)}) copy-start(f32[4,104,128]{2,1,0:T(8,128)S(1)} %collective-permute-done.9.refs_0_) | copy-start | bytes 638980
  54.1 16.8 %collective-permute-start.10 = (f32[4,104,128]{2,1,0:T(8,128)S(1)}, f32[4,104,128]{2,1,0:T(8,128)S(1)}, u32[]{:S(2)}, u32[]{:S(2)}) collective-permute-start(f32[4,104,128]{2,1,0:T(8,128)S(1)} %collective-permute-done.9.refs_0_), channel_id=1, source_target_pairs={{0,2},{1,3},{2,0},{3,1},{4,6},{5,7},{6,4},{7,5},{8,10},{9,11},{10,... | collective-permute-start | bytes 638984 | tf_op jit(solution)/shard_map/ppermute | solution.py:287
  55.6 15.8 %collective-permute-start.13 = (f32[4,104,128]{2,1,0:T(8,128)S(1)}, f32[4,104,128]{2,1,0:T(8,128)S(1)}, u32[]{:S(2)}, u32[]{:S(2)}) collective-permute-start(f32[4,104,128]{2,1,0:T(8,128)S(1)} %collective-permute-done.9.refs_0_), channel_id=1, source_target_pairs={{0,1},{1,0},{2,3},{3,2},{4,5},{5,4},{6,7},{7,6},{8,9},{9,8},{10,11... | collective-permute-start | bytes 638984 | tf_op jit(solution)/shard_map/ppermute | solution.py:287
  56.9 14.6 %copy-start.3 = (f32[4,104,128]{2,1,0:T(8,128)}, f32[4,104,128]{2,1,0:T(8,128)S(1)}, u32[]{:S(2)}) copy-start(f32[4,104,128]{2,1,0:T(8,128)S(1)} %collective-permute-done.12.refs_1_) | copy-start | bytes 638980
  56.9 14.6 %collective-permute-start.14 = (f32[4,104,128]{2,1,0:T(8,128)S(1)}, f32[4,104,128]{2,1,0:T(8,128)S(1)}, u32[]{:S(2)}, u32[]{:S(2)}) collective-permute-start(f32[4,104,128]{2,1,0:T(8,128)S(1)} %collective-permute-done.12.refs_1_), channel_id=1, source_target_pairs={{0,1},{1,0},{2,3},{3,2},{4,5},{5,4},{6,7},{7,6},{8,9},{9,8},{10,11... | collective-permute-start | bytes 638984 | tf_op jit(solution)/shard_map/ppermute | solution.py:287
  70.8 20.7 %copy-start.4 = (f32[4,104,128]{2,1,0:T(8,128)}, f32[4,104,128]{2,1,0:T(8,128)S(1)}, u32[]{:S(2)}) copy-start(f32[4,104,128]{2,1,0:T(8,128)S(1)} %collective-permute-done.10.refs_0_) | copy-start | bytes 638980
  70.8 20.7 %collective-permute-start.11 = (f32[4,104,128]{2,1,0:T(8,128)S(1)}, f32[4,104,128]{2,1,0:T(8,128)S(1)}, u32[]{:S(2)}, u32[]{:S(2)}) collective-permute-start(f32[4,104,128]{2,1,0:T(8,128)S(1)} %collective-permute-done.10.refs_0_), channel_id=1, source_target_pairs={{0,1},{1,0},{2,3},{3,2},{4,5},{5,4},{6,7},{7,6},{8,9},{9,8},{10,11... | collective-permute-start | bytes 638984 | tf_op jit(solution)/shard_map/ppermute | solution.py:287
  72.1 0.7 copy-start.6
  91.6 0.7 copy-start.8
  (3 other events, 2.0 us)

commit v2 on v1

--- a/solution.py
+++ b/solution.py
@@ -17,7 +17,10 @@
 WIDE = GROUP * BLK
 TRACE_LANE = 72
 VMEM = pl.BlockSpec(memory_space=pltpu.VMEM)
+ANY = pl.BlockSpec(memory_space=pl.ANY)
 SMEM = pl.BlockSpec(memory_space=pltpu.SMEM)
+SCOPED = 52 << 20
+SMALL = pltpu.CompilerParams(vmem_limit_bytes=16 << 20)
 HIGHEST = lax.Precision.HIGHEST
 
 
@@ -89,21 +92,25 @@
     return pack(s[:MAIN, :MAIN], s[MAIN:, :MAIN], s[MAIN:, MAIN:], trace)
 
 
-def statistics_kernel(scale, at_ref, act_ref, keep_ref, send_ref):
-    z, y = at_ref[0], at_ref[1]
-    trace = partial_trace(act_ref, scale)
-
-    def emit(part, ref):
-        for j in range(GROUP):
-            s = block_statistics(act_ref, part * GROUP + j, scale)
-            write(ref, jnp.bitwise_xor(z, j), pack_whole(s, trace))
-
-    for mine in range(2):
-
-        @pl.when(y == mine)
-        def _():
-            emit(mine, keep_ref)
-            emit(1 - mine, send_ref)
+def send_kernel(scale, act_ref, send_ref, trace_ref):
+    i = lax.axis_index("dp")
+    z, y = i // 2, i % 2
+    emit(act_ref, 1 - y, z, scale, send_ref)
+    marked = (iota((8, MAIN), 0) == 0) & (iota((8, MAIN), 1) == TRACE_LANE)
+    trace_ref[...] = jnp.where(marked, partial_trace(act_ref, scale), 0.0)
+
+
+def keep_kernel(scale, act_ref, keep_ref):
+    i = lax.axis_index("dp")
+    emit(act_ref, i % 2, i // 2, scale, keep_ref)
+
+
+def emit(act_ref, part, z, scale, ref):
+    columns = pl.ds(pl.multiple_of(part * WIDE, MAIN), WIDE)
+    half = act_ref[:, columns]
+    for j in range(GROUP):
+        piece = half[:, j * BLK : (j + 1) * BLK]
+        write(ref, jnp.bitwise_xor(z, j), pack_whole(dot(piece, piece, 0, 0) * scale, 0.0))
 
 
 def statistics_plain_kernel(scale, act_ref, out_ref):
@@ -173,21 +180,22 @@
     return 0.5 * total / D + 1e-06
 
 
-def invert_kernel(own_ref, a_ref, b_ref, out_ref):
-    trace = a_ref[0:1, TRACE_LANE : TRACE_LANE + 1] + b_ref[0:1, TRACE_LANE : TRACE_LANE + 1]
-    write(out_ref, 0, invert(own_ref[...], damping(trace)))
+def invert_kernel(a_ref, b_ref, c_ref, d_ref, out_ref):
+    own = a_ref[0] + b_ref[0] + c_ref[0] + d_ref[0]
+    trace = own[HALF + REST : HALF + REST + 1, TRACE_LANE : TRACE_LANE + 1]
+    write(out_ref, 0, invert(own, damping(trace)))
 
 
 def invert_plain_kernel(total_ref, in_ref, out_ref):
     write(out_ref, 0, invert(in_ref[0], damping(total_ref[0])))
 
 
-def build_weights(packed_ref, first, z, top_ref, mid_ref, end_ref):
+def build_weights(packed_ref, z, top_ref, mid_ref, end_ref):
     top_ref[...] = jnp.zeros_like(top_ref)
     mid_ref[...] = jnp.zeros_like(mid_ref)
     end_ref[...] = jnp.zeros_like(end_ref)
     for s in range(GROUP):
-        b11, b21, b22 = unpack(packed_ref[first + jnp.bitwise_xor(z, s)])
+        b11, b21, b22 = unpack(packed_ref[jnp.bitwise_xor(z, s)])
         whole = jnp.concatenate(
             [jnp.concatenate([b11, b21.T], axis=1), jnp.concatenate([b21, b22], axis=1)], axis=0
         )
@@ -211,72 +219,90 @@
             end_ref[lo - 384 : lo - 384 + BLK, 128:256] = low[:, 32:]
 
 
-def apply_kernel(n_groups, at_ref, *refs):
-    packed = refs[:n_groups]
-    grad_ref = refs[n_groups]
-    out_ref, top_ref, mid_ref, end_ref = refs[-4:]
+def apply_kernel(first, n_groups, at_ref, *refs):
+    packed, grad_ref = refs[:n_groups], refs[n_groups]
+    out_ref, *weights, buffer, sems, piece, piece_sems = refs[-11:]
     z, live, start = at_ref[0], at_ref[1], at_ref[2]
-    which, tile = pl.program_id(0), pl.program_id(1)
+    rows = grad_ref.shape[0]
+    parts = 3 if rows % 48 == 0 else 1
+    keep = start + iota((rows, 1), 0) < live
+
+    def build(g):
+        build_weights(packed[g], z, *weights[3 * (g % 2) : 3 * (g % 2) + 3])
+
+    def copy(g, tile):
+        lo, width = 256 * tile, min(256, WIDE - 256 * tile)
+        column = pl.multiple_of(at_ref[3 + first + g] * WIDE + lo, MAIN)
+        return pltpu.make_async_copy(
+            buffer.at[g % 2, :, lo : lo + width],
+            out_ref.at[:, pl.ds(column, width)],
+            sems.at[g % 2, tile],
+        )
+
+    def fetch(g):
+        column = pl.multiple_of(at_ref[3 + first + g] * WIDE, MAIN)
+        return pltpu.make_async_copy(
+            grad_ref.at[:, pl.ds(column, WIDE)], piece.at[g], piece_sems.at[g]
+        )
+
+    def multiply(g):
+        top_ref, mid_ref, end_ref = weights[3 * (g % 2) : 3 * (g % 2) + 3]
+        for part in range(parts):
+            here = slice(part * rows // parts, (part + 1) * rows // parts)
+            x, kept = piece[g, here], keep[here]
+            left, right = x[:, :384], x[:, 128:]
+            a = dot(jnp.concatenate([left, left], axis=1), top_ref[...], 1, 0)
+            buffer[g % 2, here, 0:256] = jnp.where(kept, a, 0.0)
+        copy(g, 0).start()
+        if g + 1 < n_groups:
+            build(g + 1)
+        for part in range(parts):
+            here = slice(part * rows // parts, (part + 1) * rows // parts)
+            x, kept = piece[g, here], keep[here]
+            left, right = x[:, :384], x[:, 128:]
+            b = dot(jnp.concatenate([right, right], axis=1), mid_ref[...], 1, 0)
+            buffer[g % 2, here, 256:512] = jnp.where(kept, b, 0.0)
+            c = dot(x[:, 384:], end_ref[...], 1, 0)
+            buffer[g % 2, here, 512:640] = jnp.where(kept, c[:, :128] + c[:, 128:], 0.0)
+        copy(g, 1).start()
+        copy(g, 2).start()
+
     for g in range(n_groups):
-
-        @pl.when((tile == 0) & (which == g))
-        def _():
-            build_weights(packed[g], 0, z, top_ref, mid_ref, end_ref)
-
-    x = grad_ref[...]
-    left, right = x[:, :384], x[:, 128:]
-    rows = x.shape[0]
-    within = start + tile * rows + iota((rows, 1), 0)
-    keep = within < live
-    a = dot(jnp.concatenate([left, left], axis=1), top_ref[...], 1, 0)
-    out_ref[:, 0:256] = jnp.where(keep, a, 0.0)
-    b = dot(jnp.concatenate([right, right], axis=1), mid_ref[...], 1, 0)
-    out_ref[:, 256:512] = jnp.where(keep, b, 0.0)
-    c = dot(x[:, 384:], end_ref[...], 1, 0)
-    out_ref[:, 512:640] = jnp.where(keep, c[:, :128] + c[:, 128:], 0.0)
-
-
-def row_tile(rows):
-    for parts in range(1, rows + 1):
-        if rows % parts == 0 and rows // parts <= 432 and (rows // parts) % 16 == 0:
-            return rows // parts
-    return rows
-
-
-def apply(groups, columns, grad_rows, z, live, start, before):
+        fetch(g).start()
+    build(0)
+    for g in range(n_groups):
+        if g >= 2:
+            for tile in range(3):
+                copy(g - 2, tile).wait()
+        fetch(g).wait()
+        pl.when(start >= 0)(functools.partial(multiply, g))
+    for g in range(max(0, n_groups - 2), n_groups):
+        for tile in range(3):
+            copy(g, tile).wait()
+
+
+def apply(groups, first, at, grad_rows, before):
     rows = grad_rows.shape[0]
-    tile = row_tile(rows)
     n = len(groups)
-    at = jnp.stack([z, live, start, *columns]).astype(jnp.int32)
-
-    def column(g, t, at_ref):
-        return (t, at_ref[3 + g])
-
-    spec = pl.BlockSpec((tile, WIDE), column)
-    ins = [pl.BlockSpec((GROUP, ROWS, MAIN), lambda g, t, at_ref: (0, 0, 0))] * n + [spec]
     args = [*groups, grad_rows]
+    ins = [SMEM] + [VMEM] * n + [ANY]
     aliases = {}
     if before is not None:
-        ins.append(pl.BlockSpec(memory_space=pl.ANY))
+        ins.append(ANY)
         args.append(before)
         aliases = {1 + n + 1: 0}
     return pl.pallas_call(
-        functools.partial(apply_kernel, n),
+        functools.partial(apply_kernel, first, n),
         out_shape=jax.ShapeDtypeStruct((rows, D), jnp.float32),
-        grid_spec=pltpu.PrefetchScalarGridSpec(
-            num_scalar_prefetch=1,
-            grid=(n, rows // tile),
-            in_specs=ins,
-            out_specs=spec,
-            scratch_shapes=[
-                pltpu.VMEM((768, 256), jnp.bfloat16),
-                pltpu.VMEM((1024, 256), jnp.bfloat16),
-                pltpu.VMEM((256, 256), jnp.bfloat16),
-            ],
-        ),
+        in_specs=ins,
+        out_specs=ANY,
+        scratch_shapes=[pltpu.VMEM((k, 256), jnp.bfloat16) for k in (768, 1024, 256)] * 2
+        + [pltpu.VMEM((2, rows, WIDE), jnp.float32), pltpu.SemaphoreType.DMA((2, 3))]
+        + [pltpu.VMEM((n, rows, WIDE), jnp.bfloat16), pltpu.SemaphoreType.DMA((n,))],
         input_output_aliases=aliases,
+        compiler_params=pltpu.CompilerParams(vmem_limit_bytes=SCOPED),
         cost_estimate=pl.CostEstimate(
-            flops=4 * rows * WIDE * 256 * n, bytes_accessed=6 * rows * WIDE * n, transcendentals=0
+            flops=4 * rows * WIDE * 256 * n, bytes_accessed=4 * rows * WIDE * n, transcendentals=0
         ),
         name="apply",
     )(at, *args)
@@ -292,42 +318,47 @@
     i, g = lax.axis_index("dp"), lax.axis_index("grad")
     z, y = i // 2, i % 2
     four = jax.ShapeDtypeStruct((GROUP, ROWS, MAIN), jnp.float32)
-    keep, send = pl.pallas_call(
-        functools.partial(statistics_kernel, scale),
-        out_shape=(four, four),
-        in_specs=[SMEM, VMEM],
+    send, trace = pl.pallas_call(
+        functools.partial(send_kernel, scale),
+        out_shape=(four, jax.ShapeDtypeStruct((8, MAIN), jnp.float32)),
+        in_specs=[VMEM],
         out_specs=(VMEM, VMEM),
-        name="statistics",
-    )(jnp.stack([z, y]).astype(jnp.int32), activations)
-    half = keep + swap(send, "dp", 1)
-    own = half[0] + swap(half[1], "dp", 2) + swap(half[2], "dp", 4) + swap(half[3], "dp", 6)
-    mark = own[HALF + REST :]
-    mark = mark + swap(mark, "grad", 2)
+        compiler_params=SMALL,
+        name="statistics_send",
+    )(activations)
+    received = swap(send, "dp", 1)
+    keep = pl.pallas_call(
+        functools.partial(keep_kernel, scale),
+        out_shape=four,
+        in_specs=[VMEM],
+        out_specs=VMEM,
+        compiler_params=SMALL,
+        name="statistics_keep",
+    )(activations)
+    trace = trace + swap(trace, "grad", 1)
+    trace = trace + swap(trace, "grad", 2)
+    trace = trace + swap(trace, "dp", 1)
+    half = keep + received
+    half = half.at[:, HALF + REST :].add(trace[None])
     inverse = pl.pallas_call(
         invert_kernel,
         out_shape=jax.ShapeDtypeStruct((1, ROWS, MAIN), jnp.float32),
-        in_specs=[VMEM] * 3,
+        in_specs=[VMEM] * 4,
         out_specs=VMEM,
+        compiler_params=SMALL,
         name="invert",
-    )(own, mark, swap(mark, "grad", 1))
+    )(half[0:1], *[swap(half[e : e + 1], "dp", 2 * e) for e in range(1, 4)])
     mine = jnp.concatenate([inverse] + [swap(inverse, "dp", d) for d in (2, 4, 6)], axis=0)
     by_y, by_x, by_core = swap(mine, "dp", 1), swap(mine, "grad", 2), swap(mine, "grad", 1)
     by_xy = swap(by_y, "grad", 2)
     by_y_core, by_x_core = swap(by_y, "grad", 1), swap(by_x, "grad", 1)
     by_xy_core = swap(by_xy, "grad", 1)
-    live = live_rows[0]
-    start = i * grad_rows.shape[0]
-
-    def column(dg, dy):
-        return (g ^ dg) * 2 + (y ^ dy)
-
-    out = apply([mine, by_core], [column(0, 0), column(1, 0)], grad_rows, z, live, start, None)
-    out = apply(
-        [by_y, by_x, by_y_core, by_x_core],
-        [column(0, 1), column(2, 0), column(1, 1), column(3, 0)],
-        grad_rows, z, live, start, out,
-    )
-    return apply([by_xy, by_xy_core], [column(2, 1), column(3, 1)], grad_rows, z, live, start, out)
+    order = ((0, 0), (1, 0), (0, 1), (2, 0), (1, 1), (3, 0), (2, 1), (3, 1))
+    columns = [(g ^ dg) * 2 + (y ^ dy) for dg, dy in order]
+    at = jnp.stack([z, live_rows[0], i * grad_rows.shape[0], *columns]).astype(jnp.int32)
+    out = apply([mine, by_core], 0, at, grad_rows, None)
+    out = apply([by_y, by_x, by_y_core, by_x_core], 2, at, grad_rows, out)
+    return apply([by_xy, by_xy_core], 6, at, grad_rows, out)
 
 
 def shards_any(activations, grad_rows, live_rows):
@@ -355,9 +386,8 @@
     n = D // WIDE
     groups = [inverses[GROUP * j : GROUP * j + GROUP] for j in range(n)]
     start = lax.axis_index("dp") * grad_rows.shape[0]
-    return apply(
-        groups, [jnp.int32(j) for j in range(n)], grad_rows, jnp.int32(0), live_rows[0], start, None
-    )
+    at = jnp.stack([jnp.int32(0), live_rows[0], start, *range(n)]).astype(jnp.int32)
+    return apply(groups, 0, at, grad_rows, None)
 
 
 def solution(mesh):

time: 104 us -> 73.2 us (0.70)
  Pallas kernels: 53.8 us -> 34.7 us
  local copies, waits for them, and re-layouts: 5.17 us -> 1.19 us
  waiting for transfers between devices: 22.2 us -> 18.5 us
  other arithmetic: 2.43 us -> 0.07 us
    pallas_call x4 -> x5, Pallas kernels: 44.7 us -> 27.1 us  [the longest x3 25.4 us: apply(): pl.pallas_call(functools.partial(apply_kernel, first, n), out_shape=jax.S...]
    ppermute x16 -> x17, waiting for transfers between devices: 22.2 us -> 18.5 us  [swap(): return lax.ppermute(x, axis, [(i, i ^ mask) for i in range(size)])]
    unnamed x22 -> x2, local copies, waits for them, and re-layouts: 3.34 us -> 1.09 us
    another operation x3 -> x1, local copies, waits for them, and re-layouts: 1.81 us -> 0.09 us  [shards_small(): jnp.stack([z, live_rows[0], i * grad_rows.shape[0], *columns])]
    pallas_call x1, Pallas kernels: 9.13 us -> 7.66 us  [shards_small(): pl.pallas_call(invert_kernel, out_shape=jax.ShapeDtypeStruct((1, ROWS, MA...]
    ppermute x16 -> x17, starting transfers between devices: 18.5 us -> 17.6 us  [swap(): return lax.ppermute(x, axis, [(i, i ^ mask) for i in range(size)])]
  transfers between devices with their start and end apart: 16 -> 17, of which waited for: 10 -> 9; matrix products, arithmetic and copies ran while one was open for 2% -> 0% of each run, Pallas kernels for 29% -> 26%
where the time goes in v2:
time: 73.2 us; the launch traced here: 73 us
  Pallas kernels  34.7 us (47%)
  waiting for transfers between devices  18.5 us (25%)
  starting transfers between devices  17.6 us (24%)
  local copies, waits for them, and re-layouts  1.19 us (2%)
  between operations  0.9 us (1%)
    pallas_call x3, Pallas kernels, apply(): pl.pallas_call(functools.partial(apply_kernel, first, n), out_shape=jax.S...  25.4 us
    ppermute x17, waiting for transfers between devices, swap(): return lax.ppermute(x, axis, [(i, i ^ mask) for i in range(size)])  18.5 us
    ppermute x17, starting transfers between devices, swap(): return lax.ppermute(x, axis, [(i, i ^ mask) for i in range(size)])  17.6 us
    pallas_call x1, Pallas kernels, shards_small(): pl.pallas_call(invert_kernel, out_shape=jax.ShapeDtypeStruct((1, ROWS, MA...  7.66 us
  transfers between devices with their start and end apart: 17, of which 9 were waited for; matrix products, arithmetic and copies ran while one was open for 0% of the time, Pallas kernels for 26%

profile of v2, /device:TPU:0, one launch (start us, length us, event | category | flops | bytes accessed | tf_op | source)
XLA Modules:
  0.0 73.0 jit_solution(18111321971810785097)
XLA Ops:
  0.0 1.1 %copy-done = bf16[256,1280]{1,0:T(8,128)(2,1)S(1)} copy-done((bf16[256,1280]{1,0:T(8,128)(2,1)S(1)}, bf16[256,1280]{1,0:T(8,128)(2,1)}, u32[]{:S(2)}) %copy-start) | copy-done | bytes 655384
  1.1 0.7 %statistics_send.1 = (f32[4,104,128]{2,1,0:T(8,128)S(1)}, f32[8,128]{1,0:T(8,128)S(1)}) custom-call(bf16[256,1280]{1,0:T(8,128)(2,1)S(1)} %copy-done), custom_call_target="tpu_custom_call" | custom-call | tf_op jit(solution)/shard_map/statistics_send/pallas_call | solution.py:321
  1.8 3.0 %collective-permute-start = (f32[4,104,128]{2,1,0:T(8,128)S(1)}, f32[4,104,128]{2,1,0:T(8,128)S(1)}, u32[]{:S(2)}, u32[]{:S(2)}) collective-permute-start(f32[4,104,128]{2,1,0:T(8,128)S(1)} %get-tuple-element.19), channel_id=1, source_target_pairs={{0,4},{4,0},{8,12},{12,8},{16,20},{20,16},{24,28},{28,24},{1,5},{5... | collective-permute-start | bytes 638984 | tf_op jit(solution)/shard_map/ppermute | solution.py:313
  4.9 1.2 %collective-permute-done.1 = f32[8,128]{1,0:T(8,128)S(1)} collective-permute-done((f32[8,128]{1,0:T(8,128)S(1)}, f32[8,128]{1,0:T(8,128)S(1)}, u32[]{:S(2)}, u32[]{:S(2)}) %collective-permute-start.1) | collective-permute-done | bytes 4128 | tf_op jit(solution)/shard_map/ppermute | solution.py:313
  6.0 1.5 %collective-permute-start.2 = (f32[8,128]{1,0:T(8,128)S(1)}, f32[8,128]{1,0:T(8,128)S(1)}, u32[]{:S(2)}, u32[]{:S(2)}) collective-permute-start(f32[8,128]{1,0:T(8,128)S(1)} %add.58), channel_id=1, source_target_pairs={{0,2},{1,3},{2,0},{3,1},{4,6},{5,7},{6,4},{7,5},{8,10},{9,11},{10,... | collective-permute-start | bytes 12296 | tf_op jit(solution)/shard_map/ppermute | solution.py:313
  7.5 2.1 %collective-permute-done.2 = f32[8,128]{1,0:T(8,128)S(1)} collective-permute-done((f32[8,128]{1,0:T(8,128)S(1)}, f32[8,128]{1,0:T(8,128)S(1)}, u32[]{:S(2)}, u32[]{:S(2)}) %collective-permute-start.2) | collective-permute-done | bytes 4128 | tf_op jit(solution)/shard_map/ppermute | solution.py:313
  9.7 0.9 %statistics_keep.1 = f32[4,104,128]{2,1,0:T(8,128)S(1)} custom-call(bf16[256,1280]{1,0:T(8,128)(2,1)S(1)} %copy-done), custom_call_target="tpu_custom_call" | custom-call | tf_op jit(solution)/shard_map/statistics_keep/pallas_call | solution.py:330
  10.6 2.6 %collective-permute-done.3 = f32[8,128]{1,0:T(8,128)S(1)} collective-permute-done((f32[8,128]{1,0:T(8,128)S(1)}, f32[8,128]{1,0:T(8,128)S(1)}, u32[]{:S(2)}, u32[]{:S(2)}) %collective-permute-start.3) | collective-permute-done | bytes 4128 | tf_op jit(solution)/shard_map/ppermute | solution.py:313
  13.3 1.6 %collective-permute-start.4 = (f32[1,104,128]{2,1,0:T(8,128)S(1)}, f32[1,104,128]{2,1,0:T(8,128)S(1)}, u32[]{:S(2)}, u32[]{:S(2)}) collective-permute-start(f32[1,104,128]{2,1,0:T(8,128)S(1)} %get-tuple-element.23), channel_id=1, source_target_pairs={{0,8},{4,12},{8,0},{12,4},{16,24},{20,28},{24,16},{28,20},{1,9},{5... | collective-permute-start | bytes 159752 | tf_op jit(solution)/shard_map/ppermute | solution.py:313
  15.0 2.6 %collective-permute-start.5 = (f32[1,104,128]{2,1,0:T(8,128)S(1)}, f32[1,104,128]{2,1,0:T(8,128)S(1)}, u32[]{:S(2)}, u32[]{:S(2)}) collective-permute-start(f32[1,104,128]{2,1,0:T(8,128)S(1)} %get-tuple-element.22), channel_id=1, source_target_pairs={{0,16},{4,20},{8,24},{12,28},{16,0},{20,4},{24,8},{28,12},{1,17},{... | collective-permute-start | bytes 159752 | tf_op jit(solution)/shard_map/ppermute | solution.py:313
  17.8 3.4 %collective-permute-done.5.c_ref = f32[1,104,128]{2,1,0:T(8,128)S(1)} collective-permute-done((f32[1,104,128]{2,1,0:T(8,128)S(1)}, f32[1,104,128]{2,1,0:T(8,128)S(1)}, u32[]{:S(2)}, u32[]{:S(2)}) %collective-permute-start.5) | collective-permute-done | bytes 53280 | tf_op jit(solution)/shard_map/ppermute | solution.py:313
  21.1 2.3 %collective-permute-done.6.d_ref = f32[1,104,128]{2,1,0:T(8,128)S(1)} collective-permute-done((f32[1,104,128]{2,1,0:T(8,128)S(1)}, f32[1,104,128]{2,1,0:T(8,128)S(1)}, u32[]{:S(2)}, u32[]{:S(2)}) %collective-permute-start.6) | collective-permute-done | bytes 53280 | tf_op jit(solution)/shard_map/ppermute | solution.py:313
  23.5 7.7 %invert.1 = f32[1,104,128]{2,1,0:T(8,128)S(1)} custom-call(f32[1,104,128]{2,1,0:T(8,128)S(1)} %get-tuple-element.24.a_ref, f32[1,104,128]{2,1,0:T(8,128)S(1)} %collective-permute-done.4.b_ref, f32[1,104,128]{2,1,0:T(8,128)S(1)} %collective-permute-done.5.c_ref, f32[1,104,128]{2,1,0:T(8,128)S(1)} %collective-permute-done.6.d_ref), custom_call_target="tpu_custom_call" | custom-call | tf_op jit(solution)/shard_map/invert/pallas_call | solution.py:343
  31.2 1.2 %collective-permute-start.8 = (f32[1,104,128]{2,1,0:T(8,128)S(1)}, f32[1,104,128]{2,1,0:T(8,128)S(1)}, u32[]{:S(2)}, u32[]{:S(2)}) collective-permute-start(f32[1,104,128]{2,1,0:T(8,128)S(1)} %invert.1), channel_id=1, source_target_pairs={{0,16},{4,20},{8,24},{12,28},{16,0},{20,4},{24,8},{28,12},{1,17},{... | collective-permute-start | bytes 159752 | tf_op jit(solution)/shard_map/ppermute | solution.py:313
  32.5 3.1 %collective-permute-start.9 = (f32[1,104,128]{2,1,0:T(8,128)S(1)}, f32[1,104,128]{2,1,0:T(8,128)S(1)}, u32[]{:S(2)}, u32[]{:S(2)}) collective-permute-start(f32[1,104,128]{2,1,0:T(8,128)S(1)} %invert.1), channel_id=1, source_target_pairs={{0,24},{4,28},{8,16},{12,20},{16,8},{20,12},{24,0},{28,4},{1,25},{... | collective-permute-start | bytes 159752 | tf_op jit(solution)/shard_map/ppermute | solution.py:313
  35.6 0.7 collective-permute-done.8
  36.3 2.1 %collective-permute-done.9 = f32[1,104,128]{2,1,0:T(8,128)S(1)} collective-permute-done((f32[1,104,128]{2,1,0:T(8,128)S(1)}, f32[1,104,128]{2,1,0:T(8,128)S(1)}, u32[]{:S(2)}, u32[]{:S(2)}) %collective-permute-start.9) | collective-permute-done | bytes 53280 | tf_op jit(solution)/shard_map/ppermute | solution.py:313
  38.4 0.6 collective-permute-start.10
  39.0 1.5 %collective-permute-start.13 = (f32[4,104,128]{2,1,0:T(8,128)S(1)}, f32[4,104,128]{2,1,0:T(8,128)S(1)}, u32[]{:S(2)}, u32[]{:S(2)}) collective-permute-start(f32[4,104,128]{2,1,0:T(8,128)S(1)} %pad_maximum_fusion.refs_0_), channel_id=1, source_target_pairs={{0,2},{1,3},{2,0},{3,1},{4,6},{5,7},{6,4},{7,5},{8,10},{9,11},{10,... | collective-permute-start | bytes 638984 | tf_op jit(solution)/shard_map/ppermute | solution.py:313
  40.5 3.8 %collective-permute-done.10.refs_0_ = f32[4,104,128]{2,1,0:T(8,128)S(1)} collective-permute-done((f32[4,104,128]{2,1,0:T(8,128)S(1)}, f32[4,104,128]{2,1,0:T(8,128)S(1)}, u32[]{:S(2)}, u32[]{:S(2)}) %collective-permute-start.10) | collective-permute-done | bytes 213024 | tf_op jit(solution)/shard_map/ppermute | solution.py:313
  44.3 1.5 %collective-permute-start.11 = (f32[4,104,128]{2,1,0:T(8,128)S(1)}, f32[4,104,128]{2,1,0:T(8,128)S(1)}, u32[]{:S(2)}, u32[]{:S(2)}) collective-permute-start(f32[4,104,128]{2,1,0:T(8,128)S(1)} %collective-permute-done.10.refs_0_), channel_id=1, source_target_pairs={{0,2},{1,3},{2,0},{3,1},{4,6},{5,7},{6,4},{7,5},{8,10},{9,11},{10,... | collective-permute-start | bytes 638984 | tf_op jit(solution)/shard_map/ppermute | solution.py:313
  47.1 7.4 %apply.3.refs_5_ = f32[1296,5120]{1,0:T(8,128)} custom-call(s32[11]{0:T(128)S(1)} %stack.43.at_ref, f32[4,104,128]{2,1,0:T(8,128)S(1)} %pad_maximum_fusion.refs_0_, f32[4,104,128]{2,1,0:T(8,128)S(1)} %collective-permute-done.16.refs_1_, bf16[1296,5120]{1,0:T(8,128)(2,1)} %refs_2_.3), custom_call_target="tpu_custom_call" | custom-call | flops 1698693120 | bytes 6635520 | tf_op jit(solution)/shard_map/apply/pallas_call | solution.py:294
  54.8 10.7 %apply.4.refs_3_ = f32[1296,5120]{1,0:T(8,128)} custom-call(s32[11]{0:T(128)S(1)} %stack.43.at_ref, f32[4,104,128]{2,1,0:T(8,128)S(1)} %collective-permute-done.10.refs_0_, f32[4,104,128]{2,1,0:T(8,128)S(1)} %collective-permute-done.13.refs_1_, f32[4,104,128]{2,1,0:T(8,128)S(1)} %collective-permute-done.14.refs_2_, ...), custom_call_target="tpu_custom_call", output_to_operand_aliasing={{}: (6, {})} | custom-call | flops 3397386240 | bytes 13271040 | tf_op jit(solution)/shard_map/apply/pallas_call | solution.py:294
  65.5 7.4 %apply.5 = f32[1296,5120]{1,0:T(8,128)} custom-call(s32[11]{0:T(128)S(1)} %stack.43.at_ref, f32[4,104,128]{2,1,0:T(8,128)S(1)} %collective-permute-done.11.refs_0_, f32[4,104,128]{2,1,0:T(8,128)S(1)} %collective-permute-done.12.refs_1_, bf16[1296,5120]{1,0:T(8,128)(2,1)} %refs_2_.3, f32[1296,5120]{1,0:T(8,128)} %apply.4.refs_3_), custom_call_target="tpu_custom_call", output_to_operand_aliasing={{}: (4, {})} | custom-call | flops 1698693120 | bytes 6635520 | tf_op jit(solution)/shard_map/apply/pallas_call | solution.py:294
  (26 shorter events, 1.4 us)
Async XLA Ops:
  0.0 1.1 %copy-start = (bf16[256,1280]{1,0:T(8,128)(2,1)S(1)}, bf16[256,1280]{1,0:T(8,128)(2,1)}, u32[]{:S(2)}) copy-start(bf16[256,1280]{1,0:T(8,128)(2,1)} %act_ref.3) | copy-start | bytes 1966084
  1.8 11.4 %collective-permute-start = (f32[4,104,128]{2,1,0:T(8,128)S(1)}, f32[4,104,128]{2,1,0:T(8,128)S(1)}, u32[]{:S(2)}, u32[]{:S(2)}) collective-permute-start(f32[4,104,128]{2,1,0:T(8,128)S(1)} %get-tuple-element.19), channel_id=1, source_target_pairs={{0,4},{4,0},{8,12},{12,8},{16,20},{20,16},{24,28},{28,24},{1,5},{5... | collective-permute-start | bytes 638984 | tf_op jit(solution)/shard_map/ppermute | solution.py:313
  4.8 1.2 %collective-permute-start.1 = (f32[8,128]{1,0:T(8,128)S(1)}, f32[8,128]{1,0:T(8,128)S(1)}, u32[]{:S(2)}, u32[]{:S(2)}) collective-permute-start(f32[8,128]{1,0:T(8,128)S(1)} %get-tuple-element.20), channel_id=1, source_target_pairs={{0,1},{1,0},{2,3},{3,2},{4,5},{5,4},{6,7},{7,6},{8,9},{9,8},{10,11... | collective-permute-start | bytes 12296 | tf_op jit(solution)/shard_map/ppermute | solution.py:313
  6.0 3.6 %collective-permute-start.2 = (f32[8,128]{1,0:T(8,128)S(1)}, f32[8,128]{1,0:T(8,128)S(1)}, u32[]{:S(2)}, u32[]{:S(2)}) collective-permute-start(f32[8,128]{1,0:T(8,128)S(1)} %add.58), channel_id=1, source_target_pairs={{0,2},{1,3},{2,0},{3,1},{4,6},{5,7},{6,4},{7,5},{8,10},{9,11},{10,... | collective-permute-start | bytes 12296 | tf_op jit(solution)/shard_map/ppermute | solution.py:313
  9.6 3.6 %collective-permute-start.3 = (f32[8,128]{1,0:T(8,128)S(1)}, f32[8,128]{1,0:T(8,128)S(1)}, u32[]{:S(2)}, u32[]{:S(2)}) collective-permute-start(f32[8,128]{1,0:T(8,128)S(1)} %add.59), channel_id=1, source_target_pairs={{0,4},{4,0},{8,12},{12,8},{16,20},{20,16},{24,28},{28,24},{1,5},{5... | collective-permute-start | bytes 12296 | tf_op jit(solution)/shard_map/ppermute | solution.py:313
  13.3 4.5 %collective-permute-start.4 = (f32[1,104,128]{2,1,0:T(8,128)S(1)}, f32[1,104,128]{2,1,0:T(8,128)S(1)}, u32[]{:S(2)}, u32[]{:S(2)}) collective-permute-start(f32[1,104,128]{2,1,0:T(8,128)S(1)} %get-tuple-element.23), channel_id=1, source_target_pairs={{0,8},{4,12},{8,0},{12,4},{16,24},{20,28},{24,16},{28,20},{1,9},{5... | collective-permute-start | bytes 159752 | tf_op jit(solution)/shard_map/ppermute | solution.py:313
  15.0 6.2 %collective-permute-start.5 = (f32[1,104,128]{2,1,0:T(8,128)S(1)}, f32[1,104,128]{2,1,0:T(8,128)S(1)}, u32[]{:S(2)}, u32[]{:S(2)}) collective-permute-start(f32[1,104,128]{2,1,0:T(8,128)S(1)} %get-tuple-element.22), channel_id=1, source_target_pairs={{0,16},{4,20},{8,24},{12,28},{16,0},{20,4},{24,8},{28,12},{1,17},{... | collective-permute-start | bytes 159752 | tf_op jit(solution)/shard_map/ppermute | solution.py:313
  17.5 5.9 %collective-permute-start.6 = (f32[1,104,128]{2,1,0:T(8,128)S(1)}, f32[1,104,128]{2,1,0:T(8,128)S(1)}, u32[]{:S(2)}, u32[]{:S(2)}) collective-permute-start(f32[1,104,128]{2,1,0:T(8,128)S(1)} %get-tuple-element.21), channel_id=1, source_target_pairs={{0,24},{4,28},{8,16},{12,20},{16,8},{20,12},{24,0},{28,4},{1,25},{... | collective-permute-start | bytes 159752 | tf_op jit(solution)/shard_map/ppermute | solution.py:313
  31.1 4.5 %collective-permute-start.7 = (f32[1,104,128]{2,1,0:T(8,128)S(1)}, f32[1,104,128]{2,1,0:T(8,128)S(1)}, u32[]{:S(2)}, u32[]{:S(2)}) collective-permute-start(f32[1,104,128]{2,1,0:T(8,128)S(1)} %invert.1), channel_id=1, source_target_pairs={{0,8},{4,12},{8,0},{12,4},{16,24},{20,28},{24,16},{28,20},{1,9},{5... | collective-permute-start | bytes 159752 | tf_op jit(solution)/shard_map/ppermute | solution.py:313
  31.2 5.1 %collective-permute-start.8 = (f32[1,104,128]{2,1,0:T(8,128)S(1)}, f32[1,104,128]{2,1,0:T(8,128)S(1)}, u32[]{:S(2)}, u32[]{:S(2)}) collective-permute-start(f32[1,104,128]{2,1,0:T(8,128)S(1)} %invert.1), channel_id=1, source_target_pairs={{0,16},{4,20},{8,24},{12,28},{16,0},{20,4},{24,8},{28,12},{1,17},{... | collective-permute-start | bytes 159752 | tf_op jit(solution)/shard_map/ppermute | solution.py:313
  32.5 5.9 %collective-permute-start.9 = (f32[1,104,128]{2,1,0:T(8,128)S(1)}, f32[1,104,128]{2,1,0:T(8,128)S(1)}, u32[]{:S(2)}, u32[]{:S(2)}) collective-permute-start(f32[1,104,128]{2,1,0:T(8,128)S(1)} %invert.1), channel_id=1, source_target_pairs={{0,24},{4,28},{8,16},{12,20},{16,8},{20,12},{24,0},{28,4},{1,25},{... | collective-permute-start | bytes 159752 | tf_op jit(solution)/shard_map/ppermute | solution.py:313
  38.4 5.9 %collective-permute-start.10 = (f32[4,104,128]{2,1,0:T(8,128)S(1)}, f32[4,104,128]{2,1,0:T(8,128)S(1)}, u32[]{:S(2)}, u32[]{:S(2)}) collective-permute-start(f32[4,104,128]{2,1,0:T(8,128)S(1)} %pad_maximum_fusion.refs_0_), channel_id=1, source_target_pairs={{0,4},{4,0},{8,12},{12,8},{16,20},{20,16},{24,28},{28,24},{1,5},{5... | collective-permute-start | bytes 638984 | tf_op jit(solution)/shard_map/ppermute | solution.py:313
  39.0 7.1 %collective-permute-start.13 = (f32[4,104,128]{2,1,0:T(8,128)S(1)}, f32[4,104,128]{2,1,0:T(8,128)S(1)}, u32[]{:S(2)}, u32[]{:S(2)}) collective-permute-start(f32[4,104,128]{2,1,0:T(8,128)S(1)} %pad_maximum_fusion.refs_0_), channel_id=1, source_target_pairs={{0,2},{1,3},{2,0},{3,1},{4,6},{5,7},{6,4},{7,5},{8,10},{9,11},{10,... | collective-permute-start | bytes 638984 | tf_op jit(solution)/shard_map/ppermute | solution.py:313
  40.5 6.6 %collective-permute-start.16 = (f32[4,104,128]{2,1,0:T(8,128)S(1)}, f32[4,104,128]{2,1,0:T(8,128)S(1)}, u32[]{:S(2)}, u32[]{:S(2)}) collective-permute-start(f32[4,104,128]{2,1,0:T(8,128)S(1)} %pad_maximum_fusion.refs_0_), channel_id=1, source_target_pairs={{0,1},{1,0},{2,3},{3,2},{4,5},{5,4},{6,7},{7,6},{8,9},{9,8},{10,11... | collective-permute-start | bytes 638984 | tf_op jit(solution)/shard_map/ppermute | solution.py:313
  44.3 10.1 %collective-permute-start.11 = (f32[4,104,128]{2,1,0:T(8,128)S(1)}, f32[4,104,128]{2,1,0:T(8,128)S(1)}, u32[]{:S(2)}, u32[]{:S(2)}) collective-permute-start(f32[4,104,128]{2,1,0:T(8,128)S(1)} %collective-permute-done.10.refs_0_), channel_id=1, source_target_pairs={{0,2},{1,3},{2,0},{3,1},{4,6},{5,7},{6,4},{7,5},{8,10},{9,11},{10,... | collective-permute-start | bytes 638984 | tf_op jit(solution)/shard_map/ppermute | solution.py:313
  45.8 9.0 %collective-permute-start.14 = (f32[4,104,128]{2,1,0:T(8,128)S(1)}, f32[4,104,128]{2,1,0:T(8,128)S(1)}, u32[]{:S(2)}, u32[]{:S(2)}) collective-permute-start(f32[4,104,128]{2,1,0:T(8,128)S(1)} %collective-permute-done.10.refs_0_), channel_id=1, source_target_pairs={{0,1},{1,0},{2,3},{3,2},{4,5},{5,4},{6,7},{7,6},{8,9},{9,8},{10,11... | collective-permute-start | bytes 638984 | tf_op jit(solution)/shard_map/ppermute | solution.py:313
  46.1 8.7 %collective-permute-start.15 = (f32[4,104,128]{2,1,0:T(8,128)S(1)}, f32[4,104,128]{2,1,0:T(8,128)S(1)}, u32[]{:S(2)}, u32[]{:S(2)}) collective-permute-start(f32[4,104,128]{2,1,0:T(8,128)S(1)} %collective-permute-done.13.refs_1_), channel_id=1, source_target_pairs={{0,1},{1,0},{2,3},{3,2},{4,5},{5,4},{6,7},{7,6},{8,9},{9,8},{10,11... | collective-permute-start | bytes 638984 | tf_op jit(solution)/shard_map/ppermute | solution.py:313
  54.4 11.0 %collective-permute-start.12 = (f32[4,104,128]{2,1,0:T(8,128)S(1)}, f32[4,104,128]{2,1,0:T(8,128)S(1)}, u32[]{:S(2)}, u32[]{:S(2)}) collective-permute-start(f32[4,104,128]{2,1,0:T(8,128)S(1)} %collective-permute-done.11.refs_0_), channel_id=1, source_target_pairs={{0,1},{1,0},{2,3},{3,2},{4,5},{5,4},{6,7},{7,6},{8,9},{9,8},{10,11... | collective-permute-start | bytes 638984 | tf_op jit(solution)/shard_map/ppermute | solution.py:313

commit v3 on v2

--- a/solution.py
+++ b/solution.py
@@ -190,45 +190,49 @@
     write(out_ref, 0, invert(in_ref[0], damping(total_ref[0])))
 
 
-def build_weights(packed_ref, z, top_ref, mid_ref, end_ref):
+def halves(packed_ref, place):
+    b11, b21, b22 = unpack(packed_ref[place])
+    whole = jnp.concatenate(
+        [jnp.concatenate([b11, b21.T], axis=1), jnp.concatenate([b21, b22], axis=1)], axis=0
+    )
+    high = whole.astype(jnp.bfloat16)
+    return high, (whole - high.astype(jnp.float32)).astype(jnp.bfloat16)
+
+
+def build_first(packed_ref, z, top_ref, mid_ref):
     top_ref[...] = jnp.zeros_like(top_ref)
     mid_ref[...] = jnp.zeros_like(mid_ref)
+    for at, part in zip((0, 384), halves(packed_ref, z)):
+        top_ref[at : at + BLK, 0:BLK] = part
+    for at, part in zip((0, 384), halves(packed_ref, jnp.bitwise_xor(z, 1))):
+        top_ref[at + BLK : at + 2 * BLK, BLK:256] = part[:, : 256 - BLK]
+    for at, part in zip((0, 512), halves(packed_ref, jnp.bitwise_xor(z, 1))):
+        mid_ref[at + 32 : at + 32 + BLK, 0:64] = part[:, 96:]
+
+
+def build_rest(packed_ref, z, mid_ref, end_ref):
     end_ref[...] = jnp.zeros_like(end_ref)
-    for s in range(GROUP):
-        b11, b21, b22 = unpack(packed_ref[jnp.bitwise_xor(z, s)])
-        whole = jnp.concatenate(
-            [jnp.concatenate([b11, b21.T], axis=1), jnp.concatenate([b21, b22], axis=1)], axis=0
-        )
-        high = whole.astype(jnp.bfloat16)
-        low = (whole - high.astype(jnp.float32)).astype(jnp.bfloat16)
-        lo = s * BLK
-        if s < 2:
-            cut = min(256 - lo, BLK)
-            top_ref[lo : lo + BLK, lo : lo + cut] = high[:, :cut]
-            top_ref[384 + lo : 384 + lo + BLK, lo : lo + cut] = low[:, :cut]
-        if s == 1:
-            mid_ref[lo - 128 : lo - 128 + BLK, 0 : lo + BLK - 256] = high[:, 256 - lo :]
-            mid_ref[384 + lo : 384 + lo + BLK, 0 : lo + BLK - 256] = low[:, 256 - lo :]
-        if s == 2:
-            mid_ref[lo - 128 : lo - 128 + BLK, lo - 256 : lo - 256 + BLK] = high
-            mid_ref[384 + lo : 384 + lo + BLK, lo - 256 : lo - 256 + BLK] = low
-        if s == 3:
-            mid_ref[lo - 128 : lo - 128 + BLK, lo - 256 : 256] = high[:, :32]
-            mid_ref[384 + lo : 384 + lo + BLK, lo - 256 : 256] = low[:, :32]
-            end_ref[lo - 384 : lo - 384 + BLK, 0:128] = high[:, 32:]
-            end_ref[lo - 384 : lo - 384 + BLK, 128:256] = low[:, 32:]
+    for at, part in zip((0, 512), halves(packed_ref, jnp.bitwise_xor(z, 2))):
+        mid_ref[at + 192 : at + 192 + BLK, 64 : 64 + BLK] = part
+    for at, part in zip((0, 512), halves(packed_ref, jnp.bitwise_xor(z, 3))):
+        mid_ref[at + 352 : at + 352 + BLK, 224:256] = part[:, :32]
+        end_ref[96 : 96 + BLK, at // 4 : at // 4 + 128] = part[:, 32:]
 
 
 def apply_kernel(first, n_groups, at_ref, *refs):
     packed, grad_ref = refs[:n_groups], refs[n_groups]
-    out_ref, *weights, buffer, sems, piece, piece_sems = refs[-11:]
+    out_ref, *weights, buffer, sems, held, held_sems = refs[-11:]
     z, live, start = at_ref[0], at_ref[1], at_ref[2]
     rows = grad_ref.shape[0]
-    parts = 3 if rows % 48 == 0 else 1
+    parts = row_parts(rows)
     keep = start + iota((rows, 1), 0) < live
 
-    def build(g):
-        build_weights(packed[g], z, *weights[3 * (g % 2) : 3 * (g % 2) + 3])
+    def build(g, first_part, last_part):
+        top_ref, mid_ref, end_ref = weights[3 * (g % 2) : 3 * (g % 2) + 3]
+        if first_part:
+            build_first(packed[g], z, top_ref, mid_ref)
+        if last_part:
+            build_rest(packed[g], z, mid_ref, end_ref)
 
     def copy(g, tile):
         lo, width = 256 * tile, min(256, WIDE - 256 * tile)
@@ -241,35 +245,34 @@
 
     def fetch(g):
         column = pl.multiple_of(at_ref[3 + first + g] * WIDE, MAIN)
-        return pltpu.make_async_copy(
-            grad_ref.at[:, pl.ds(column, WIDE)], piece.at[g], piece_sems.at[g]
-        )
+        return pltpu.make_async_copy(grad_ref.at[:, pl.ds(column, WIDE)], held.at[g], held_sems.at[g])
 
     def multiply(g):
         top_ref, mid_ref, end_ref = weights[3 * (g % 2) : 3 * (g % 2) + 3]
+        if g == 0:
+            build(0, True, False)
         for part in range(parts):
             here = slice(part * rows // parts, (part + 1) * rows // parts)
-            x, kept = piece[g, here], keep[here]
-            left, right = x[:, :384], x[:, 128:]
+            left = held[g, here, 0:384]
             a = dot(jnp.concatenate([left, left], axis=1), top_ref[...], 1, 0)
-            buffer[g % 2, here, 0:256] = jnp.where(kept, a, 0.0)
+            buffer[g % 2, here, 0:256] = jnp.where(keep[here], a, 0.0)
         copy(g, 0).start()
+        if g == 0:
+            build(0, False, True)
         if g + 1 < n_groups:
-            build(g + 1)
+            build(g + 1, True, True)
         for part in range(parts):
             here = slice(part * rows // parts, (part + 1) * rows // parts)
-            x, kept = piece[g, here], keep[here]
-            left, right = x[:, :384], x[:, 128:]
+            kept, right, end = keep[here], held[g, here, 128:640], held[g, here, 384:640]
             b = dot(jnp.concatenate([right, right], axis=1), mid_ref[...], 1, 0)
             buffer[g % 2, here, 256:512] = jnp.where(kept, b, 0.0)
-            c = dot(x[:, 384:], end_ref[...], 1, 0)
+            c = dot(end, end_ref[...], 1, 0)
             buffer[g % 2, here, 512:640] = jnp.where(kept, c[:, :128] + c[:, 128:], 0.0)
         copy(g, 1).start()
         copy(g, 2).start()
 
     for g in range(n_groups):
         fetch(g).start()
-    build(0)
     for g in range(n_groups):
         if g >= 2:
             for tile in range(3):
@@ -279,6 +282,10 @@
     for g in range(max(0, n_groups - 2), n_groups):
         for tile in range(3):
             copy(g, tile).wait()
+
+
+def row_parts(rows):
+    return 3 if rows % 48 == 0 else 1
 
 
 def apply(groups, first, at, grad_rows, before):
@@ -350,15 +357,17 @@
     )(half[0:1], *[swap(half[e : e + 1], "dp", 2 * e) for e in range(1, 4)])
     mine = jnp.concatenate([inverse] + [swap(inverse, "dp", d) for d in (2, 4, 6)], axis=0)
     by_y, by_x, by_core = swap(mine, "dp", 1), swap(mine, "grad", 2), swap(mine, "grad", 1)
-    by_xy = swap(by_y, "grad", 2)
-    by_y_core, by_x_core = swap(by_y, "grad", 1), swap(by_x, "grad", 1)
-    by_xy_core = swap(by_xy, "grad", 1)
     order = ((0, 0), (1, 0), (0, 1), (2, 0), (1, 1), (3, 0), (2, 1), (3, 1))
     columns = [(g ^ dg) * 2 + (y ^ dy) for dg, dy in order]
     at = jnp.stack([z, live_rows[0], i * grad_rows.shape[0], *columns]).astype(jnp.int32)
-    out = apply([mine, by_core], 0, at, grad_rows, None)
-    out = apply([by_y, by_x, by_y_core, by_x_core], 2, at, grad_rows, out)
-    return apply([by_xy, by_xy_core], 6, at, grad_rows, out)
+    out = apply([mine], 0, at, grad_rows, None)
+    by_y, out = lax.optimization_barrier((by_y, out))
+    by_xy = swap(by_y, "grad", 2)
+    by_y_core, by_x_core = swap(by_y, "grad", 1), swap(by_x, "grad", 1)
+    out = apply([by_core, by_y, by_x], 1, at, grad_rows, out)
+    by_xy, out = lax.optimization_barrier((by_xy, out))
+    by_xy_core = swap(by_xy, "grad", 1)
+    return apply([by_y_core, by_x_core, by_xy, by_xy_core], 4, at, grad_rows, out)
 
 
 def shards_any(activations, grad_rows, live_rows):

time: 73.2 us -> 69.1 us (0.944)
  waiting for transfers between devices: 18.5 us -> 14.1 us
  Pallas kernels: 34.7 us -> 35.7 us
    ppermute x17, waiting for transfers between devices: 18.5 us -> 14.1 us  [swap(): return lax.ppermute(x, axis, [(i, i ^ mask) for i in range(size)])]
    pallas_call x3, Pallas kernels: 25.4 us -> 26.4 us  [apply(): pl.pallas_call(functools.partial(apply_kernel, first, n), out_shape=jax.S...]
  transfers between devices with their start and end apart: 17 -> 17, of which waited for: 9 -> 9; matrix products, arithmetic and copies ran while one was open for 0% -> 0% of each run, Pallas kernels for 26% -> 23%
where the time goes in v3:
time: 69.1 us; the launch traced here: 68.9 us
  Pallas kernels  35.7 us (52%)
  starting transfers between devices  17 us (25%)
  waiting for transfers between devices  14.1 us (20%)
  local copies, waits for them, and re-layouts  1.19 us (2%)
  between operations  0.9 us (1%)
    pallas_call x3, Pallas kernels, apply(): pl.pallas_call(functools.partial(apply_kernel, first, n), out_shape=jax.S...  26.4 us
    ppermute x17, starting transfers between devices, swap(): return lax.ppermute(x, axis, [(i, i ^ mask) for i in range(size)])  17 us
    ppermute x17, waiting for transfers between devices, swap(): return lax.ppermute(x, axis, [(i, i ^ mask) for i in range(size)])  14.1 us
    pallas_call x1, Pallas kernels, shards_small(): pl.pallas_call(invert_kernel, out_shape=jax.ShapeDtypeStruct((1, ROWS, MA...  7.66 us
  transfers between devices with their start and end apart: 17, of which 9 were waited for; matrix products, arithmetic and copies ran while one was open for 0% of the time, Pallas kernels for 23%

profile of v3, /device:TPU:0, one launch (start us, length us, event | category | flops | bytes accessed | tf_op | source)
XLA Modules:
  0.0 68.9 jit_solution(6469058941885686977)
XLA Ops:
  0.0 1.1 %copy-done = bf16[256,1280]{1,0:T(8,128)(2,1)S(1)} copy-done((bf16[256,1280]{1,0:T(8,128)(2,1)S(1)}, bf16[256,1280]{1,0:T(8,128)(2,1)}, u32[]{:S(2)}) %copy-start) | copy-done | bytes 655384
  1.1 0.7 %statistics_send.1 = (f32[4,104,128]{2,1,0:T(8,128)S(1)}, f32[8,128]{1,0:T(8,128)S(1)}) custom-call(bf16[256,1280]{1,0:T(8,128)(2,1)S(1)} %copy-done), custom_call_target="tpu_custom_call" | custom-call | tf_op jit(solution)/shard_map/statistics_send/pallas_call | solution.py:328
  1.8 3.0 %collective-permute-start = (f32[4,104,128]{2,1,0:T(8,128)S(1)}, f32[4,104,128]{2,1,0:T(8,128)S(1)}, u32[]{:S(2)}, u32[]{:S(2)}) collective-permute-start(f32[4,104,128]{2,1,0:T(8,128)S(1)} %get-tuple-element.23), channel_id=1, source_target_pairs={{0,4},{4,0},{8,12},{12,8},{16,20},{20,16},{24,28},{28,24},{1,5},{5... | collective-permute-start | bytes 638984 | tf_op jit(solution)/shard_map/ppermute | solution.py:320
  4.9 1.2 %collective-permute-done.1 = f32[8,128]{1,0:T(8,128)S(1)} collective-permute-done((f32[8,128]{1,0:T(8,128)S(1)}, f32[8,128]{1,0:T(8,128)S(1)}, u32[]{:S(2)}, u32[]{:S(2)}) %collective-permute-start.1) | collective-permute-done | bytes 4128 | tf_op jit(solution)/shard_map/ppermute | solution.py:320
  6.0 1.5 %collective-permute-start.2 = (f32[8,128]{1,0:T(8,128)S(1)}, f32[8,128]{1,0:T(8,128)S(1)}, u32[]{:S(2)}, u32[]{:S(2)}) collective-permute-start(f32[8,128]{1,0:T(8,128)S(1)} %add.58), channel_id=1, source_target_pairs={{0,2},{1,3},{2,0},{3,1},{4,6},{5,7},{6,4},{7,5},{8,10},{9,11},{10,... | collective-permute-start | bytes 12296 | tf_op jit(solution)/shard_map/ppermute | solution.py:320
  7.5 2.1 %collective-permute-done.2 = f32[8,128]{1,0:T(8,128)S(1)} collective-permute-done((f32[8,128]{1,0:T(8,128)S(1)}, f32[8,128]{1,0:T(8,128)S(1)}, u32[]{:S(2)}, u32[]{:S(2)}) %collective-permute-start.2) | collective-permute-done | bytes 4128 | tf_op jit(solution)/shard_map/ppermute | solution.py:320
  9.7 0.9 %statistics_keep.1 = f32[4,104,128]{2,1,0:T(8,128)S(1)} custom-call(bf16[256,1280]{1,0:T(8,128)(2,1)S(1)} %copy-done), custom_call_target="tpu_custom_call" | custom-call | tf_op jit(solution)/shard_map/statistics_keep/pallas_call | solution.py:337
  10.6 2.6 %collective-permute-done.3 = f32[8,128]{1,0:T(8,128)S(1)} collective-permute-done((f32[8,128]{1,0:T(8,128)S(1)}, f32[8,128]{1,0:T(8,128)S(1)}, u32[]{:S(2)}, u32[]{:S(2)}) %collective-permute-start.3) | collective-permute-done | bytes 4128 | tf_op jit(solution)/shard_map/ppermute | solution.py:320
  13.3 3.7 %collective-permute-start.6 = (f32[1,104,128]{2,1,0:T(8,128)S(1)}, f32[1,104,128]{2,1,0:T(8,128)S(1)}, u32[]{:S(2)}, u32[]{:S(2)}) collective-permute-start(f32[1,104,128]{2,1,0:T(8,128)S(1)} %get-tuple-element.29), channel_id=1, source_target_pairs={{0,24},{4,28},{8,16},{12,20},{16,8},{20,12},{24,0},{28,4},{1,25},{... | collective-permute-start | bytes 159752 | tf_op jit(solution)/shard_map/ppermute | solution.py:320
  17.0 0.8 %collective-permute-start.4 = (f32[1,104,128]{2,1,0:T(8,128)S(1)}, f32[1,104,128]{2,1,0:T(8,128)S(1)}, u32[]{:S(2)}, u32[]{:S(2)}) collective-permute-start(f32[1,104,128]{2,1,0:T(8,128)S(1)} %get-tuple-element.31), channel_id=1, source_target_pairs={{0,8},{4,12},{8,0},{12,4},{16,24},{20,28},{24,16},{28,20},{1,9},{5... | collective-permute-start | bytes 159752 | tf_op jit(solution)/shard_map/ppermute | solution.py:320
  17.8 1.6 %collective-permute-done.6.d_ref = f32[1,104,128]{2,1,0:T(8,128)S(1)} collective-permute-done((f32[1,104,128]{2,1,0:T(8,128)S(1)}, f32[1,104,128]{2,1,0:T(8,128)S(1)}, u32[]{:S(2)}, u32[]{:S(2)}) %collective-permute-start.6) | collective-permute-done | bytes 53280 | tf_op jit(solution)/shard_map/ppermute | solution.py:320
  19.4 2.6 %collective-permute-done.5.c_ref = f32[1,104,128]{2,1,0:T(8,128)S(1)} collective-permute-done((f32[1,104,128]{2,1,0:T(8,128)S(1)}, f32[1,104,128]{2,1,0:T(8,128)S(1)}, u32[]{:S(2)}, u32[]{:S(2)}) %collective-permute-start.5) | collective-permute-done | bytes 53280 | tf_op jit(solution)/shard_map/ppermute | solution.py:320
  22.0 7.7 %invert.1 = f32[1,104,128]{2,1,0:T(8,128)S(1)} custom-call(f32[1,104,128]{2,1,0:T(8,128)S(1)} %get-tuple-element.32.a_ref, f32[1,104,128]{2,1,0:T(8,128)S(1)} %collective-permute-done.4.b_ref, f32[1,104,128]{2,1,0:T(8,128)S(1)} %collective-permute-done.5.c_ref, f32[1,104,128]{2,1,0:T(8,128)S(1)} %collective-permute-done.6.d_ref), custom_call_target="tpu_custom_call" | custom-call | tf_op jit(solution)/shard_map/invert/pallas_call | solution.py:350
  29.7 1.5 %collective-permute-start.9 = (f32[1,104,128]{2,1,0:T(8,128)S(1)}, f32[1,104,128]{2,1,0:T(8,128)S(1)}, u32[]{:S(2)}, u32[]{:S(2)}) collective-permute-start(f32[1,104,128]{2,1,0:T(8,128)S(1)} %invert.1), channel_id=1, source_target_pairs={{0,24},{4,28},{8,16},{12,20},{16,8},{20,12},{24,0},{28,4},{1,25},{... | collective-permute-start | bytes 159752 | tf_op jit(solution)/shard_map/ppermute | solution.py:320
  31.2 0.6 collective-permute-start.8
  31.9 2.3 %collective-permute-start.7 = (f32[1,104,128]{2,1,0:T(8,128)S(1)}, f32[1,104,128]{2,1,0:T(8,128)S(1)}, u32[]{:S(2)}, u32[]{:S(2)}) collective-permute-start(f32[1,104,128]{2,1,0:T(8,128)S(1)} %invert.1), channel_id=1, source_target_pairs={{0,8},{4,12},{8,0},{12,4},{16,24},{20,28},{24,16},{28,20},{1,9},{5... | collective-permute-start | bytes 159752 | tf_op jit(solution)/shard_map/ppermute | solution.py:320
  34.1 1.5 %collective-permute-done.9 = f32[1,104,128]{2,1,0:T(8,128)S(1)} collective-permute-done((f32[1,104,128]{2,1,0:T(8,128)S(1)}, f32[1,104,128]{2,1,0:T(8,128)S(1)}, u32[]{:S(2)}, u32[]{:S(2)}) %collective-permute-start.9) | collective-permute-done | bytes 53280 | tf_op jit(solution)/shard_map/ppermute | solution.py:320
  35.7 0.6 collective-permute-done.8
  37.4 1.5 %collective-permute-start.12 = (f32[4,104,128]{2,1,0:T(8,128)S(1)}, f32[4,104,128]{2,1,0:T(8,128)S(1)}, u32[]{:S(2)}, u32[]{:S(2)}) collective-permute-start(f32[4,104,128]{2,1,0:T(8,128)S(1)} %pad_maximum_fusion.refs_0_), channel_id=1, source_target_pairs={{0,2},{1,3},{2,0},{3,1},{4,6},{5,7},{6,4},{7,5},{8,10},{9,11},{10,... | collective-permute-start | bytes 638984 | tf_op jit(solution)/shard_map/ppermute | solution.py:320
  39.7 5.6 %apply.3.refs_4_ = f32[1296,5120]{1,0:T(8,128)} custom-call(s32[11]{0:T(128)S(1)} %stack.43.at_ref, f32[4,104,128]{2,1,0:T(8,128)S(1)} %pad_maximum_fusion.refs_0_, bf16[1296,5120]{1,0:T(8,128)(2,1)} %refs_4_.1), custom_call_target="tpu_custom_call" | custom-call | flops 849346560 | bytes 3317760 | tf_op jit(solution)/shard_map/apply/pallas_call | solution.py:301
  45.3 0.6 collective-permute-start.14
  46.4 9.6 %apply.4.refs_5_ = f32[1296,5120]{1,0:T(8,128)} custom-call(s32[11]{0:T(128)S(1)} %stack.43.at_ref, f32[4,104,128]{2,1,0:T(8,128)S(1)} %collective-permute-done.15.refs_0_, f32[4,104,128]{2,1,0:T(8,128)S(1)} %collective-permute-done.10.refs_1_, f32[4,104,128]{2,1,0:T(8,128)S(1)} %collective-permute-done.12.refs_2_, ...), custom_call_target="tpu_custom_call", output_to_operand_aliasing={{}: (5, {})} | custom-call | flops 2548039680 | bytes 9953280 | tf_op jit(solution)/shard_map/apply/pallas_call | solution.py:301
  56.3 1.2 %collective-permute-done.16.refs_3_ = f32[4,104,128]{2,1,0:T(8,128)S(1)} collective-permute-done((f32[4,104,128]{2,1,0:T(8,128)S(1)}, f32[4,104,128]{2,1,0:T(8,128)S(1)}, u32[]{:S(2)}, u32[]{:S(2)}) %collective-permute-start.16) | collective-permute-done | bytes 213024 | tf_op jit(solution)/shard_map/ppermute | solution.py:320
  57.5 11.2 %apply.5 = f32[1296,5120]{1,0:T(8,128)} custom-call(s32[11]{0:T(128)S(1)} %stack.43.at_ref, f32[4,104,128]{2,1,0:T(8,128)S(1)} %collective-permute-done.11.refs_0_, f32[4,104,128]{2,1,0:T(8,128)S(1)} %collective-permute-done.13.refs_1_, f32[4,104,128]{2,1,0:T(8,128)S(1)} %collective-permute-done.14.refs_2_, ...), custom_call_target="tpu_custom_call", output_to_operand_aliasing={{}: (6, {})} | custom-call | flops 3397386240 | bytes 13271040 | tf_op jit(solution)/shard_map/apply/pallas_call | solution.py:301
  (26 shorter events, 2.2 us)
Async XLA Ops:
  0.0 1.1 %copy-start = (bf16[256,1280]{1,0:T(8,128)(2,1)S(1)}, bf16[256,1280]{1,0:T(8,128)(2,1)}, u32[]{:S(2)}) copy-start(bf16[256,1280]{1,0:T(8,128)(2,1)} %act_ref.3) | copy-start | bytes 1966084
  1.8 11.4 %collective-permute-start = (f32[4,104,128]{2,1,0:T(8,128)S(1)}, f32[4,104,128]{2,1,0:T(8,128)S(1)}, u32[]{:S(2)}, u32[]{:S(2)}) collective-permute-start(f32[4,104,128]{2,1,0:T(8,128)S(1)} %get-tuple-element.23), channel_id=1, source_target_pairs={{0,4},{4,0},{8,12},{12,8},{16,20},{20,16},{24,28},{28,24},{1,5},{5... | collective-permute-start | bytes 638984 | tf_op jit(solution)/shard_map/ppermute | solution.py:320
  4.8 1.2 %collective-permute-start.1 = (f32[8,128]{1,0:T(8,128)S(1)}, f32[8,128]{1,0:T(8,128)S(1)}, u32[]{:S(2)}, u32[]{:S(2)}) collective-permute-start(f32[8,128]{1,0:T(8,128)S(1)} %get-tuple-element.24), channel_id=1, source_target_pairs={{0,1},{1,0},{2,3},{3,2},{4,5},{5,4},{6,7},{7,6},{8,9},{9,8},{10,11... | collective-permute-start | bytes 12296 | tf_op jit(solution)/shard_map/ppermute | solution.py:320
  6.0 3.6 %collective-permute-start.2 = (f32[8,128]{1,0:T(8,128)S(1)}, f32[8,128]{1,0:T(8,128)S(1)}, u32[]{:S(2)}, u32[]{:S(2)}) collective-permute-start(f32[8,128]{1,0:T(8,128)S(1)} %add.58), channel_id=1, source_target_pairs={{0,2},{1,3},{2,0},{3,1},{4,6},{5,7},{6,4},{7,5},{8,10},{9,11},{10,... | collective-permute-start | bytes 12296 | tf_op jit(solution)/shard_map/ppermute | solution.py:320
  9.6 3.6 %collective-permute-start.3 = (f32[8,128]{1,0:T(8,128)S(1)}, f32[8,128]{1,0:T(8,128)S(1)}, u32[]{:S(2)}, u32[]{:S(2)}) collective-permute-start(f32[8,128]{1,0:T(8,128)S(1)} %add.59), channel_id=1, source_target_pairs={{0,4},{4,0},{8,12},{12,8},{16,20},{20,16},{24,28},{28,24},{1,5},{5... | collective-permute-start | bytes 12296 | tf_op jit(solution)/shard_map/ppermute | solution.py:320
  13.3 6.1 %collective-permute-start.6 = (f32[1,104,128]{2,1,0:T(8,128)S(1)}, f32[1,104,128]{2,1,0:T(8,128)S(1)}, u32[]{:S(2)}, u32[]{:S(2)}) collective-permute-start(f32[1,104,128]{2,1,0:T(8,128)S(1)} %get-tuple-element.29), channel_id=1, source_target_pairs={{0,24},{4,28},{8,16},{12,20},{16,8},{20,12},{24,0},{28,4},{1,25},{... | collective-permute-start | bytes 159752 | tf_op jit(solution)/shard_map/ppermute | solution.py:320
  17.0 5.0 %collective-permute-start.5 = (f32[1,104,128]{2,1,0:T(8,128)S(1)}, f32[1,104,128]{2,1,0:T(8,128)S(1)}, u32[]{:S(2)}, u32[]{:S(2)}) collective-permute-start(f32[1,104,128]{2,1,0:T(8,128)S(1)} %get-tuple-element.30), channel_id=1, source_target_pairs={{0,16},{4,20},{8,24},{12,28},{16,0},{20,4},{24,8},{28,12},{1,17},{... | collective-permute-start | bytes 159752 | tf_op jit(solution)/shard_map/ppermute | solution.py:320
  17.0 5.0 %collective-permute-start.4 = (f32[1,104,128]{2,1,0:T(8,128)S(1)}, f32[1,104,128]{2,1,0:T(8,128)S(1)}, u32[]{:S(2)}, u32[]{:S(2)}) collective-permute-start(f32[1,104,128]{2,1,0:T(8,128)S(1)} %get-tuple-element.31), channel_id=1, source_target_pairs={{0,8},{4,12},{8,0},{12,4},{16,24},{20,28},{24,16},{28,20},{1,9},{5... | collective-permute-start | bytes 159752 | tf_op jit(solution)/shard_map/ppermute | solution.py:320
  29.7 6.0 %collective-permute-start.9 = (f32[1,104,128]{2,1,0:T(8,128)S(1)}, f32[1,104,128]{2,1,0:T(8,128)S(1)}, u32[]{:S(2)}, u32[]{:S(2)}) collective-permute-start(f32[1,104,128]{2,1,0:T(8,128)S(1)} %invert.1), channel_id=1, source_target_pairs={{0,24},{4,28},{8,16},{12,20},{16,8},{20,12},{24,0},{28,4},{1,25},{... | collective-permute-start | bytes 159752 | tf_op jit(solution)/shard_map/ppermute | solution.py:320
  31.2 5.1 %collective-permute-start.8 = (f32[1,104,128]{2,1,0:T(8,128)S(1)}, f32[1,104,128]{2,1,0:T(8,128)S(1)}, u32[]{:S(2)}, u32[]{:S(2)}) collective-permute-start(f32[1,104,128]{2,1,0:T(8,128)S(1)} %invert.1), channel_id=1, source_target_pairs={{0,16},{4,20},{8,24},{12,28},{16,0},{20,4},{24,8},{28,12},{1,17},{... | collective-permute-start | bytes 159752 | tf_op jit(solution)/shard_map/ppermute | solution.py:320
  31.9 5.0 %collective-permute-start.7 = (f32[1,104,128]{2,1,0:T(8,128)S(1)}, f32[1,104,128]{2,1,0:T(8,128)S(1)}, u32[]{:S(2)}, u32[]{:S(2)}) collective-permute-start(f32[1,104,128]{2,1,0:T(8,128)S(1)} %invert.1), channel_id=1, source_target_pairs={{0,8},{4,12},{8,0},{12,4},{16,24},{20,28},{24,16},{28,20},{1,9},{5... | collective-permute-start | bytes 159752 | tf_op jit(solution)/shard_map/ppermute | solution.py:320
  36.8 8.4 %collective-permute-start.10 = (f32[4,104,128]{2,1,0:T(8,128)S(1)}, f32[4,104,128]{2,1,0:T(8,128)S(1)}, u32[]{:S(2)}, u32[]{:S(2)}) collective-permute-start(f32[4,104,128]{2,1,0:T(8,128)S(1)} %pad_maximum_fusion.refs_0_), channel_id=1, source_target_pairs={{0,4},{4,0},{8,12},{12,8},{16,20},{20,16},{24,28},{28,24},{1,5},{5... | collective-permute-start | bytes 638984 | tf_op jit(solution)/shard_map/ppermute | solution.py:320
  37.4 8.7 %collective-permute-start.12 = (f32[4,104,128]{2,1,0:T(8,128)S(1)}, f32[4,104,128]{2,1,0:T(8,128)S(1)}, u32[]{:S(2)}, u32[]{:S(2)}) collective-permute-start(f32[4,104,128]{2,1,0:T(8,128)S(1)} %pad_maximum_fusion.refs_0_), channel_id=1, source_target_pairs={{0,2},{1,3},{2,0},{3,1},{4,6},{5,7},{6,4},{7,5},{8,10},{9,11},{10,... | collective-permute-start | bytes 638984 | tf_op jit(solution)/shard_map/ppermute | solution.py:320
  38.9 7.5 %collective-permute-start.15 = (f32[4,104,128]{2,1,0:T(8,128)S(1)}, f32[4,104,128]{2,1,0:T(8,128)S(1)}, u32[]{:S(2)}, u32[]{:S(2)}) collective-permute-start(f32[4,104,128]{2,1,0:T(8,128)S(1)} %pad_maximum_fusion.refs_0_), channel_id=1, source_target_pairs={{0,1},{1,0},{2,3},{3,2},{4,5},{5,4},{6,7},{7,6},{8,9},{9,8},{10,11... | collective-permute-start | bytes 638984 | tf_op jit(solution)/shard_map/ppermute | solution.py:320
  45.3 10.7 %collective-permute-start.14 = (f32[4,104,128]{2,1,0:T(8,128)S(1)}, f32[4,104,128]{2,1,0:T(8,128)S(1)}, u32[]{:S(2)}, u32[]{:S(2)}) collective-permute-start(f32[4,104,128]{2,1,0:T(8,128)S(1)} %collective-permute-done.10.refs_1_), channel_id=1, source_target_pairs={{0,2},{1,3},{2,0},{3,1},{4,6},{5,7},{6,4},{7,5},{8,10},{9,11},{10,... | collective-permute-start | bytes 638984 | tf_op jit(solution)/shard_map/ppermute | solution.py:320
  45.9 10.4 %collective-permute-start.11 = (f32[4,104,128]{2,1,0:T(8,128)S(1)}, f32[4,104,128]{2,1,0:T(8,128)S(1)}, u32[]{:S(2)}, u32[]{:S(2)}) collective-permute-start(f32[4,104,128]{2,1,0:T(8,128)S(1)} %collective-permute-done.10.refs_1_), channel_id=1, source_target_pairs={{0,1},{1,0},{2,3},{3,2},{4,5},{5,4},{6,7},{7,6},{8,9},{9,8},{10,11... | collective-permute-start | bytes 638984 | tf_op jit(solution)/shard_map/ppermute | solution.py:320
  46.1 10.2 %collective-permute-start.13 = (f32[4,104,128]{2,1,0:T(8,128)S(1)}, f32[4,104,128]{2,1,0:T(8,128)S(1)}, u32[]{:S(2)}, u32[]{:S(2)}) collective-permute-start(f32[4,104,128]{2,1,0:T(8,128)S(1)} %collective-permute-done.12.refs_2_), channel_id=1, source_target_pairs={{0,1},{1,0},{2,3},{3,2},{4,5},{5,4},{6,7},{7,6},{8,9},{9,8},{10,11... | collective-permute-start | bytes 638984 | tf_op jit(solution)/shard_map/ppermute | solution.py:320
  56.0 1.5 %collective-permute-start.16 = (f32[4,104,128]{2,1,0:T(8,128)S(1)}, f32[4,104,128]{2,1,0:T(8,128)S(1)}, u32[]{:S(2)}, u32[]{:S(2)}) collective-permute-start(f32[4,104,128]{2,1,0:T(8,128)S(1)} %collective-permute-done.14.refs_2_), channel_id=1, source_target_pairs={{0,1},{1,0},{2,3},{3,2},{4,5},{5,4},{6,7},{7,6},{8,9},{9,8},{10,11... | collective-permute-start | bytes 638984 | tf_op jit(solution)/shard_map/ppermute | solution.py:320

commit v4 on v3

--- a/solution.py
+++ b/solution.py
@@ -19,7 +19,6 @@
 VMEM = pl.BlockSpec(memory_space=pltpu.VMEM)
 ANY = pl.BlockSpec(memory_space=pl.ANY)
 SMEM = pl.BlockSpec(memory_space=pltpu.SMEM)
-SCOPED = 52 << 20
 SMALL = pltpu.CompilerParams(vmem_limit_bytes=16 << 20)
 HIGHEST = lax.Precision.HIGHEST
 
@@ -133,18 +132,19 @@
             jnp.where(inside, jnp.where(lane == k + i, 1.0, 0.0), spread(t[i : i + 1, :]))
             for i in range(8)
         ]
-        small = [[spread(t[i : i + 1, k + j : k + j + 1]) for j in range(8)] for i in range(8)]
+        small = {(i, j): spread(t[i : i + 1, k + j : k + j + 1]) for i in range(8) for j in range(i, 8)}
         for a in range(8):
-            pivot = 1.0 / small[a][a]
+            pivot = 1.0 / small[a, a]
             rows[a] = rows[a] * pivot
-            for b in range(a + 1, 8):
-                small[a][b] = small[a][b] * pivot
+            scaled = {b: small[a, b] * pivot for b in range(a + 1, 8)}
             for c in range(8):
                 if c != a:
-                    factor = small[c][a]
+                    factor = small[min(a, c), max(a, c)]
                     rows[c] = rows[c] - factor * rows[a]
-                    for b in range(a + 1, 8):
-                        small[c][b] = small[c][b] - factor * small[a][b]
+                    for b in range(max(a + 1, c), 8):
+                        small[c, b] = small[c, b] - factor * scaled[b]
+            for b in scaled:
+                small[a, b] = scaled[b]
         rows = [jnp.where(inside, -x, x) for x in rows]
         for j in range(len(tiles)):
             total = None
@@ -219,11 +219,18 @@
         end_ref[96 : 96 + BLK, at // 4 : at // 4 + 128] = part[:, 32:]
 
 
-def apply_kernel(first, n_groups, at_ref, *refs):
-    packed, grad_ref = refs[:n_groups], refs[n_groups]
-    out_ref, *weights, buffer, sems, held, held_sems = refs[-11:]
+def apply_kernel(first, n_groups, fetched, at_ref, *refs):
+    packed = refs[:n_groups]
+    if fetched:
+        held = refs[n_groups : 2 * n_groups]
+        out_ref, *weights, buffer, sems = refs[-9:]
+        incoming = []
+    else:
+        out_ref, *weights, buffer, sems, room, room_sems = refs[-11:]
+        held = [room.at[g] for g in range(n_groups)]
+        incoming = piece_copies(at_ref, first, refs[n_groups], held, room_sems)
     z, live, start = at_ref[0], at_ref[1], at_ref[2]
-    rows = grad_ref.shape[0]
+    rows = held[0].shape[0]
     parts = row_parts(rows)
     keep = start + iota((rows, 1), 0) < live
 
@@ -243,17 +250,13 @@
             sems.at[g % 2, tile],
         )
 
-    def fetch(g):
-        column = pl.multiple_of(at_ref[3 + first + g] * WIDE, MAIN)
-        return pltpu.make_async_copy(grad_ref.at[:, pl.ds(column, WIDE)], held.at[g], held_sems.at[g])
-
     def multiply(g):
         top_ref, mid_ref, end_ref = weights[3 * (g % 2) : 3 * (g % 2) + 3]
         if g == 0:
             build(0, True, False)
         for part in range(parts):
             here = slice(part * rows // parts, (part + 1) * rows // parts)
-            left = held[g, here, 0:384]
+            left = held[g][here, 0:384]
             a = dot(jnp.concatenate([left, left], axis=1), top_ref[...], 1, 0)
             buffer[g % 2, here, 0:256] = jnp.where(keep[here], a, 0.0)
         copy(g, 0).start()
@@ -263,7 +266,7 @@
             build(g + 1, True, True)
         for part in range(parts):
             here = slice(part * rows // parts, (part + 1) * rows // parts)
-            kept, right, end = keep[here], held[g, here, 128:640], held[g, here, 384:640]
+            kept, right, end = keep[here], held[g][here, 128:640], held[g][here, 384:640]
             b = dot(jnp.concatenate([right, right], axis=1), mid_ref[...], 1, 0)
             buffer[g % 2, here, 256:512] = jnp.where(kept, b, 0.0)
             c = dot(end, end_ref[...], 1, 0)
@@ -271,13 +274,14 @@
         copy(g, 1).start()
         copy(g, 2).start()
 
+    for arrival in incoming:
+        arrival.start()
     for g in range(n_groups):
-        fetch(g).start()
-    for g in range(n_groups):
+        if incoming:
+            incoming[g].wait()
         if g >= 2:
             for tile in range(3):
                 copy(g - 2, tile).wait()
-        fetch(g).wait()
         pl.when(start >= 0)(functools.partial(multiply, g))
     for g in range(max(0, n_groups - 2), n_groups):
         for tile in range(3):
@@ -288,31 +292,52 @@
     return 3 if rows % 48 == 0 else 1
 
 
-def apply(groups, first, at, grad_rows, before):
+def apply(groups, first, at, pieces, grad_rows, before):
     rows = grad_rows.shape[0]
     n = len(groups)
-    args = [*groups, grad_rows]
-    ins = [SMEM] + [VMEM] * n + [ANY]
+    fetched = pieces is not None
+    given = pieces if fetched else [grad_rows]
+    args = [*groups, *given]
+    ins = [SMEM] + [VMEM] * n + ([VMEM] * n if fetched else [ANY])
+    scratch = [pltpu.VMEM((k, 256), jnp.bfloat16) for k in (768, 1024, 256)] * 2
+    scratch += [pltpu.VMEM((2, rows, WIDE), jnp.float32), pltpu.SemaphoreType.DMA((2, 3))]
+    if not fetched:
+        scratch += [pltpu.VMEM((n, rows, WIDE), grad_rows.dtype), pltpu.SemaphoreType.DMA((n,))]
     aliases = {}
     if before is not None:
         ins.append(ANY)
         args.append(before)
-        aliases = {1 + n + 1: 0}
+        aliases = {len(args): 0}
     return pl.pallas_call(
-        functools.partial(apply_kernel, first, n),
+        functools.partial(apply_kernel, first, n, fetched),
         out_shape=jax.ShapeDtypeStruct((rows, D), jnp.float32),
         in_specs=ins,
         out_specs=ANY,
-        scratch_shapes=[pltpu.VMEM((k, 256), jnp.bfloat16) for k in (768, 1024, 256)] * 2
-        + [pltpu.VMEM((2, rows, WIDE), jnp.float32), pltpu.SemaphoreType.DMA((2, 3))]
-        + [pltpu.VMEM((n, rows, WIDE), jnp.bfloat16), pltpu.SemaphoreType.DMA((n,))],
+        scratch_shapes=scratch,
         input_output_aliases=aliases,
-        compiler_params=pltpu.CompilerParams(vmem_limit_bytes=SCOPED),
+        compiler_params=pltpu.CompilerParams(vmem_limit_bytes=(20 if fetched else 52) << 20),
         cost_estimate=pl.CostEstimate(
             flops=4 * rows * WIDE * 256 * n, bytes_accessed=4 * rows * WIDE * n, transcendentals=0
         ),
         name="apply",
     )(at, *args)
+
+
+def piece_copies(at_ref, first, grad_ref, pieces, sems):
+    rows, copies = grad_ref.shape[0], []
+    for g, piece in enumerate(pieces):
+        column = pl.multiple_of(at_ref[3 + first + g] * WIDE, MAIN)
+        source = grad_ref.at[0:rows, pl.ds(column, WIDE)]
+        copies.append(pltpu.make_async_copy(source, piece, sems.at[g]))
+    return copies
+
+
+def fetch_kernel(at_ref, grad_ref, *refs):
+    copies = piece_copies(at_ref, 0, grad_ref, refs[:-1], refs[-1])
+    for copy in copies:
+        copy.start()
+    for copy in copies:
+        copy.wait()
 
 
 def swap(x, axis, mask):
@@ -347,6 +372,21 @@
     trace = trace + swap(trace, "dp", 1)
     half = keep + received
     half = half.at[:, HALF + REST :].add(trace[None])
+    order = ((0, 0), (1, 0), (0, 1), (2, 0), (1, 1), (3, 0), (2, 1), (3, 1))
+    columns = [(g ^ dg) * 2 + (y ^ dy) for dg, dy in order]
+    at = jnp.stack([z, live_rows[0], i * grad_rows.shape[0], *columns]).astype(jnp.int32)
+    n = 1
+    pieces = pl.pallas_call(
+        fetch_kernel,
+        out_shape=[jax.ShapeDtypeStruct((grad_rows.shape[0], WIDE), grad_rows.dtype)] * n,
+        in_specs=[SMEM, ANY],
+        out_specs=[VMEM] * n,
+        scratch_shapes=[pltpu.SemaphoreType.DMA((n,))],
+        compiler_params=pltpu.CompilerParams(vmem_limit_bytes=50 << 20),
+        cost_estimate=pl.CostEstimate(flops=0, bytes_accessed=grad_rows.size // 4, transcendentals=0),
+        name="fetch",
+    )(at, grad_rows)
+    parts = [half[0:1], *[swap(half[e : e + 1], "dp", 2 * e) for e in range(1, 4)]]
     inverse = pl.pallas_call(
         invert_kernel,
         out_shape=jax.ShapeDtypeStruct((1, ROWS, MAIN), jnp.float32),
@@ -354,20 +394,19 @@
         out_specs=VMEM,
         compiler_params=SMALL,
         name="invert",
-    )(half[0:1], *[swap(half[e : e + 1], "dp", 2 * e) for e in range(1, 4)])
-    mine = jnp.concatenate([inverse] + [swap(inverse, "dp", d) for d in (2, 4, 6)], axis=0)
+    )(*parts)
+    others = [swap(inverse, "dp", d) for d in (2, 4, 6)]
+    others[0], pieces = lax.optimization_barrier((others[0], pieces))
+    mine = jnp.concatenate([inverse, *others], axis=0)
     by_y, by_x, by_core = swap(mine, "dp", 1), swap(mine, "grad", 2), swap(mine, "grad", 1)
-    order = ((0, 0), (1, 0), (0, 1), (2, 0), (1, 1), (3, 0), (2, 1), (3, 1))
-    columns = [(g ^ dg) * 2 + (y ^ dy) for dg, dy in order]
-    at = jnp.stack([z, live_rows[0], i * grad_rows.shape[0], *columns]).astype(jnp.int32)
-    out = apply([mine], 0, at, grad_rows, None)
+    out = apply([mine], 0, at, pieces, grad_rows, None)
     by_y, out = lax.optimization_barrier((by_y, out))
     by_xy = swap(by_y, "grad", 2)
     by_y_core, by_x_core = swap(by_y, "grad", 1), swap(by_x, "grad", 1)
-    out = apply([by_core, by_y, by_x], 1, at, grad_rows, out)
+    out = apply([by_core, by_y, by_x], 1, at, None, grad_rows, out)
     by_xy, out = lax.optimization_barrier((by_xy, out))
     by_xy_core = swap(by_xy, "grad", 1)
-    return apply([by_y_core, by_x_core, by_xy, by_xy_core], 4, at, grad_rows, out)
+    return apply([by_y_core, by_x_core, by_xy, by_xy_core], 4, at, None, grad_rows, out)
 
 
 def shards_any(activations, grad_rows, live_rows):
@@ -396,7 +435,7 @@
     groups = [inverses[GROUP * j : GROUP * j + GROUP] for j in range(n)]
     start = lax.axis_index("dp") * grad_rows.shape[0]
     at = jnp.stack([jnp.int32(0), live_rows[0], start, *range(n)]).astype(jnp.int32)
-    return apply(groups, 0, at, grad_rows, None)
+    return apply(groups, 0, at, None, grad_rows, None)
 
 
 def solution(mesh):

time: 69.1 us -> 68.2 us (0.987)
  starting transfers between devices: 17 us -> 16.3 us
    ppermute x17, starting transfers between devices: 17 us -> 16.3 us  [swap(): return lax.ppermute(x, axis, [(i, i ^ mask) for i in range(size)])]
    pallas_call x3 -> x4, Pallas kernels: 26.4 us -> 27.1 us  [the longest x3 25.1 us: apply(): pl.pallas_call(functools.partial(apply_kernel, first, n, fetched), out_sh...]
  transfers between devices with their start and end apart: 17 -> 17, of which waited for: 9 -> 7; matrix products, arithmetic and copies ran while one was open for 0% -> 0% of each run, Pallas kernels for 23% -> 25%
where the time goes in v4:
time: 68.2 us; the launch traced here: 68 us
  Pallas kernels  35.7 us (52%)
  starting transfers between devices  16.3 us (24%)
  waiting for transfers between devices  13.8 us (20%)
  local copies, waits for them, and re-layouts  1.19 us (2%)
  between operations  0.94 us (1%)
    pallas_call x3, Pallas kernels, apply(): pl.pallas_call(functools.partial(apply_kernel, first, n, fetched), out_sh...  25.1 us
    ppermute x17, starting transfers between devices, swap(): return lax.ppermute(x, axis, [(i, i ^ mask) for i in range(size)])  16.3 us
    ppermute x17, waiting for transfers between devices, swap(): return lax.ppermute(x, axis, [(i, i ^ mask) for i in range(size)])  13.8 us
    pallas_call x1, Pallas kernels, shards_small(): pl.pallas_call(invert_kernel, out_shape=jax.ShapeDtypeStruct((1, ROWS, MA...  6.99 us
    pallas_call x1, Pallas kernels, shards_small(): pl.pallas_call(fetch_kernel, out_shape=[jax.ShapeDtypeStruct((grad_rows.s...  2 us
  transfers between devices with their start and end apart: 17, of which 7 were waited for; matrix products, arithmetic and copies ran while one was open for 0% of the time, Pallas kernels for 25%

profile of v4, /device:TPU:0, one launch (start us, length us, event | category | flops | bytes accessed | tf_op | source)
XLA Modules:
  0.0 68.0 jit_solution(5968582073860566561)
XLA Ops:
  0.0 1.1 %copy-done = bf16[256,1280]{1,0:T(8,128)(2,1)S(1)} copy-done((bf16[256,1280]{1,0:T(8,128)(2,1)S(1)}, bf16[256,1280]{1,0:T(8,128)(2,1)}, u32[]{:S(2)}) %copy-start) | copy-done | bytes 655384
  1.1 0.7 %statistics_send.1 = (f32[4,104,128]{2,1,0:T(8,128)S(1)}, f32[8,128]{1,0:T(8,128)S(1)}) custom-call(bf16[256,1280]{1,0:T(8,128)(2,1)S(1)} %copy-done), custom_call_target="tpu_custom_call" | custom-call | tf_op jit(solution)/shard_map/statistics_send/pallas_call | solution.py:353
  1.8 3.0 %collective-permute-start = (f32[4,104,128]{2,1,0:T(8,128)S(1)}, f32[4,104,128]{2,1,0:T(8,128)S(1)}, u32[]{:S(2)}, u32[]{:S(2)}) collective-permute-start(f32[4,104,128]{2,1,0:T(8,128)S(1)} %get-tuple-element.25), channel_id=1, source_target_pairs={{0,4},{4,0},{8,12},{12,8},{16,20},{20,16},{24,28},{28,24},{1,5},{5... | collective-permute-start | bytes 638984 | tf_op jit(solution)/shard_map/ppermute | solution.py:345
  4.9 1.2 %collective-permute-done.1 = f32[8,128]{1,0:T(8,128)S(1)} collective-permute-done((f32[8,128]{1,0:T(8,128)S(1)}, f32[8,128]{1,0:T(8,128)S(1)}, u32[]{:S(2)}, u32[]{:S(2)}) %collective-permute-start.1) | collective-permute-done | bytes 4128 | tf_op jit(solution)/shard_map/ppermute | solution.py:345
  6.0 1.5 %collective-permute-start.2 = (f32[8,128]{1,0:T(8,128)S(1)}, f32[8,128]{1,0:T(8,128)S(1)}, u32[]{:S(2)}, u32[]{:S(2)}) collective-permute-start(f32[8,128]{1,0:T(8,128)S(1)} %add.58), channel_id=1, source_target_pairs={{0,2},{1,3},{2,0},{3,1},{4,6},{5,7},{6,4},{7,5},{8,10},{9,11},{10,... | collective-permute-start | bytes 12296 | tf_op jit(solution)/shard_map/ppermute | solution.py:345
  7.5 2.1 %collective-permute-done.2 = f32[8,128]{1,0:T(8,128)S(1)} collective-permute-done((f32[8,128]{1,0:T(8,128)S(1)}, f32[8,128]{1,0:T(8,128)S(1)}, u32[]{:S(2)}, u32[]{:S(2)}) %collective-permute-start.2) | collective-permute-done | bytes 4128 | tf_op jit(solution)/shard_map/ppermute | solution.py:345
  9.7 0.9 %statistics_keep.1 = f32[4,104,128]{2,1,0:T(8,128)S(1)} custom-call(bf16[256,1280]{1,0:T(8,128)(2,1)S(1)} %copy-done), custom_call_target="tpu_custom_call" | custom-call | tf_op jit(solution)/shard_map/statistics_keep/pallas_call | solution.py:362
  10.6 2.6 %collective-permute-done.3 = f32[8,128]{1,0:T(8,128)S(1)} collective-permute-done((f32[8,128]{1,0:T(8,128)S(1)}, f32[8,128]{1,0:T(8,128)S(1)}, u32[]{:S(2)}, u32[]{:S(2)}) %collective-permute-start.3) | collective-permute-done | bytes 4128 | tf_op jit(solution)/shard_map/ppermute | solution.py:345
  13.3 3.7 %collective-permute-start.6 = (f32[1,104,128]{2,1,0:T(8,128)S(1)}, f32[1,104,128]{2,1,0:T(8,128)S(1)}, u32[]{:S(2)}, u32[]{:S(2)}) collective-permute-start(f32[1,104,128]{2,1,0:T(8,128)S(1)} %get-tuple-element.33), channel_id=1, source_target_pairs={{0,24},{4,28},{8,16},{12,20},{16,8},{20,12},{24,0},{28,4},{1,25},{... | collective-permute-start | bytes 159752 | tf_op jit(solution)/shard_map/ppermute | solution.py:345
  17.0 0.8 %collective-permute-start.4 = (f32[1,104,128]{2,1,0:T(8,128)S(1)}, f32[1,104,128]{2,1,0:T(8,128)S(1)}, u32[]{:S(2)}, u32[]{:S(2)}) collective-permute-start(f32[1,104,128]{2,1,0:T(8,128)S(1)} %get-tuple-element.35), channel_id=1, source_target_pairs={{0,8},{4,12},{8,0},{12,4},{16,24},{20,28},{24,16},{28,20},{1,9},{5... | collective-permute-start | bytes 159752 | tf_op jit(solution)/shard_map/ppermute | solution.py:345
  17.8 1.6 %collective-permute-done.6.d_ref = f32[1,104,128]{2,1,0:T(8,128)S(1)} collective-permute-done((f32[1,104,128]{2,1,0:T(8,128)S(1)}, f32[1,104,128]{2,1,0:T(8,128)S(1)}, u32[]{:S(2)}, u32[]{:S(2)}) %collective-permute-start.6) | collective-permute-done | bytes 53280 | tf_op jit(solution)/shard_map/ppermute | solution.py:345
  19.4 2.6 %collective-permute-done.5.c_ref = f32[1,104,128]{2,1,0:T(8,128)S(1)} collective-permute-done((f32[1,104,128]{2,1,0:T(8,128)S(1)}, f32[1,104,128]{2,1,0:T(8,128)S(1)}, u32[]{:S(2)}, u32[]{:S(2)}) %collective-permute-start.5) | collective-permute-done | bytes 53280 | tf_op jit(solution)/shard_map/ppermute | solution.py:345
  22.0 7.0 %invert.1 = f32[1,104,128]{2,1,0:T(8,128)S(1)} custom-call(f32[1,104,128]{2,1,0:T(8,128)S(1)} %get-tuple-element.36.a_ref, f32[1,104,128]{2,1,0:T(8,128)S(1)} %collective-permute-done.4.b_ref, f32[1,104,128]{2,1,0:T(8,128)S(1)} %collective-permute-done.5.c_ref, f32[1,104,128]{2,1,0:T(8,128)S(1)} %collective-permute-done.6.d_ref), custom_call_target="tpu_custom_call" | custom-call | tf_op jit(solution)/shard_map/invert/pallas_call | solution.py:390
  29.3 3.2 %collective-permute-start.9 = (f32[1,104,128]{2,1,0:T(8,128)S(1)}, f32[1,104,128]{2,1,0:T(8,128)S(1)}, u32[]{:S(2)}, u32[]{:S(2)}) collective-permute-start(f32[1,104,128]{2,1,0:T(8,128)S(1)} %invert.1), channel_id=1, source_target_pairs={{0,24},{4,28},{8,16},{12,20},{16,8},{20,12},{24,0},{28,4},{1,25},{... | collective-permute-start | bytes 159752 | tf_op jit(solution)/shard_map/ppermute | solution.py:345
  33.3 2.0 %fetch.1.refs_1_ = bf16[1296,640]{1,0:T(8,128)(2,1)S(1)} custom-call(s32[11]{0:T(128)S(1)} %stack.43.at_ref, bf16[1296,5120]{1,0:T(8,128)(2,1)} %refs_4_.1), custom_call_target="tpu_custom_call" | custom-call | bytes 1658880 | tf_op jit(solution)/shard_map/fetch/pallas_call | solution.py:379
  35.3 2.3 %collective-permute-done.8 = f32[1,104,128]{2,1,0:T(8,128)S(1)} collective-permute-done((f32[1,104,128]{2,1,0:T(8,128)S(1)}, f32[1,104,128]{2,1,0:T(8,128)S(1)}, u32[]{:S(2)}, u32[]{:S(2)}) %collective-permute-start.8) | collective-permute-done | bytes 53280 | tf_op jit(solution)/shard_map/ppermute | solution.py:345
  37.6 0.6 collective-permute-start.10
  38.2 1.5 %collective-permute-start.12 = (f32[4,104,128]{2,1,0:T(8,128)S(1)}, f32[4,104,128]{2,1,0:T(8,128)S(1)}, u32[]{:S(2)}, u32[]{:S(2)}) collective-permute-start(f32[4,104,128]{2,1,0:T(8,128)S(1)} %pad_maximum_fusion.refs_0_), channel_id=1, source_target_pairs={{0,2},{1,3},{2,0},{3,1},{4,6},{5,7},{6,4},{7,5},{8,10},{9,11},{10,... | collective-permute-start | bytes 638984 | tf_op jit(solution)/shard_map/ppermute | solution.py:345
  39.7 4.3 %apply.3.refs_4_ = f32[1296,5120]{1,0:T(8,128)} custom-call(s32[11]{0:T(128)S(1)} %stack.43.at_ref, f32[4,104,128]{2,1,0:T(8,128)S(1)} %pad_maximum_fusion.refs_0_, bf16[1296,640]{1,0:T(8,128)(2,1)S(1)} %fetch.1.refs_1_), custom_call_target="tpu_custom_call" | custom-call | flops 849346560 | bytes 3317760 | tf_op jit(solution)/shard_map/apply/pallas_call | solution.py:311
  44.0 1.0 %collective-permute-start.14 = (f32[4,104,128]{2,1,0:T(8,128)S(1)}, f32[4,104,128]{2,1,0:T(8,128)S(1)}, u32[]{:S(2)}, u32[]{:S(2)}) collective-permute-start(f32[4,104,128]{2,1,0:T(8,128)S(1)} %collective-permute-done.10.refs_1_), channel_id=1, source_target_pairs={{0,2},{1,3},{2,0},{3,1},{4,6},{5,7},{6,4},{7,5},{8,10},{9,11},{10,... | collective-permute-start | bytes 638984 | tf_op jit(solution)/shard_map/ppermute | solution.py:345
  45.0 0.5 collective-permute-start.13
  45.5 9.6 %apply.4.refs_5_ = f32[1296,5120]{1,0:T(8,128)} custom-call(s32[11]{0:T(128)S(1)} %stack.43.at_ref, f32[4,104,128]{2,1,0:T(8,128)S(1)} %collective-permute-done.15.refs_0_, f32[4,104,128]{2,1,0:T(8,128)S(1)} %collective-permute-done.10.refs_1_, f32[4,104,128]{2,1,0:T(8,128)S(1)} %collective-permute-done.12.refs_2_, ...), custom_call_target="tpu_custom_call", output_to_operand_aliasing={{}: (5, {})} | custom-call | flops 2548039680 | bytes 9953280 | tf_op jit(solution)/shard_map/apply/pallas_call | solution.py:311
  55.2 1.4 %collective-permute-done.16.refs_3_ = f32[4,104,128]{2,1,0:T(8,128)S(1)} collective-permute-done((f32[4,104,128]{2,1,0:T(8,128)S(1)}, f32[4,104,128]{2,1,0:T(8,128)S(1)}, u32[]{:S(2)}, u32[]{:S(2)}) %collective-permute-start.16) | collective-permute-done | bytes 213024 | tf_op jit(solution)/shard_map/ppermute | solution.py:345
  56.7 11.2 %apply.5 = f32[1296,5120]{1,0:T(8,128)} custom-call(s32[11]{0:T(128)S(1)} %stack.43.at_ref, f32[4,104,128]{2,1,0:T(8,128)S(1)} %collective-permute-done.11.refs_0_, f32[4,104,128]{2,1,0:T(8,128)S(1)} %collective-permute-done.13.refs_1_, f32[4,104,128]{2,1,0:T(8,128)S(1)} %collective-permute-done.14.refs_2_, ...), custom_call_target="tpu_custom_call", output_to_operand_aliasing={{}: (6, {})} | custom-call | flops 3397386240 | bytes 13271040 | tf_op jit(solution)/shard_map/apply/pallas_call | solution.py:311
  (27 shorter events, 0.7 us)
Async XLA Ops:
  0.0 1.1 %copy-start = (bf16[256,1280]{1,0:T(8,128)(2,1)S(1)}, bf16[256,1280]{1,0:T(8,128)(2,1)}, u32[]{:S(2)}) copy-start(bf16[256,1280]{1,0:T(8,128)(2,1)} %act_ref.3) | copy-start | bytes 1966084
  1.8 11.4 %collective-permute-start = (f32[4,104,128]{2,1,0:T(8,128)S(1)}, f32[4,104,128]{2,1,0:T(8,128)S(1)}, u32[]{:S(2)}, u32[]{:S(2)}) collective-permute-start(f32[4,104,128]{2,1,0:T(8,128)S(1)} %get-tuple-element.25), channel_id=1, source_target_pairs={{0,4},{4,0},{8,12},{12,8},{16,20},{20,16},{24,28},{28,24},{1,5},{5... | collective-permute-start | bytes 638984 | tf_op jit(solution)/shard_map/ppermute | solution.py:345
  4.8 1.2 %collective-permute-start.1 = (f32[8,128]{1,0:T(8,128)S(1)}, f32[8,128]{1,0:T(8,128)S(1)}, u32[]{:S(2)}, u32[]{:S(2)}) collective-permute-start(f32[8,128]{1,0:T(8,128)S(1)} %get-tuple-element.26), channel_id=1, source_target_pairs={{0,1},{1,0},{2,3},{3,2},{4,5},{5,4},{6,7},{7,6},{8,9},{9,8},{10,11... | collective-permute-start | bytes 12296 | tf_op jit(solution)/shard_map/ppermute | solution.py:345
  6.0 3.6 %collective-permute-start.2 = (f32[8,128]{1,0:T(8,128)S(1)}, f32[8,128]{1,0:T(8,128)S(1)}, u32[]{:S(2)}, u32[]{:S(2)}) collective-permute-start(f32[8,128]{1,0:T(8,128)S(1)} %add.58), channel_id=1, source_target_pairs={{0,2},{1,3},{2,0},{3,1},{4,6},{5,7},{6,4},{7,5},{8,10},{9,11},{10,... | collective-permute-start | bytes 12296 | tf_op jit(solution)/shard_map/ppermute | solution.py:345
  9.6 3.6 %collective-permute-start.3 = (f32[8,128]{1,0:T(8,128)S(1)}, f32[8,128]{1,0:T(8,128)S(1)}, u32[]{:S(2)}, u32[]{:S(2)}) collective-permute-start(f32[8,128]{1,0:T(8,128)S(1)} %add.59), channel_id=1, source_target_pairs={{0,4},{4,0},{8,12},{12,8},{16,20},{20,16},{24,28},{28,24},{1,5},{5... | collective-permute-start | bytes 12296 | tf_op jit(solution)/shard_map/ppermute | solution.py:345
  13.3 6.1 %collective-permute-start.6 = (f32[1,104,128]{2,1,0:T(8,128)S(1)}, f32[1,104,128]{2,1,0:T(8,128)S(1)}, u32[]{:S(2)}, u32[]{:S(2)}) collective-permute-start(f32[1,104,128]{2,1,0:T(8,128)S(1)} %get-tuple-element.33), channel_id=1, source_target_pairs={{0,24},{4,28},{8,16},{12,20},{16,8},{20,12},{24,0},{28,4},{1,25},{... | collective-permute-start | bytes 159752 | tf_op jit(solution)/shard_map/ppermute | solution.py:345
  17.0 5.0 %collective-permute-start.5 = (f32[1,104,128]{2,1,0:T(8,128)S(1)}, f32[1,104,128]{2,1,0:T(8,128)S(1)}, u32[]{:S(2)}, u32[]{:S(2)}) collective-permute-start(f32[1,104,128]{2,1,0:T(8,128)S(1)} %get-tuple-element.34), channel_id=1, source_target_pairs={{0,16},{4,20},{8,24},{12,28},{16,0},{20,4},{24,8},{28,12},{1,17},{... | collective-permute-start | bytes 159752 | tf_op jit(solution)/shard_map/ppermute | solution.py:345
  17.0 5.0 %collective-permute-start.4 = (f32[1,104,128]{2,1,0:T(8,128)S(1)}, f32[1,104,128]{2,1,0:T(8,128)S(1)}, u32[]{:S(2)}, u32[]{:S(2)}) collective-permute-start(f32[1,104,128]{2,1,0:T(8,128)S(1)} %get-tuple-element.35), channel_id=1, source_target_pairs={{0,8},{4,12},{8,0},{12,4},{16,24},{20,28},{24,16},{28,20},{1,9},{5... | collective-permute-start | bytes 159752 | tf_op jit(solution)/shard_map/ppermute | solution.py:345
  29.0 6.3 %collective-permute-start.7 = (f32[1,104,128]{2,1,0:T(8,128)S(1)}, f32[1,104,128]{2,1,0:T(8,128)S(1)}, u32[]{:S(2)}, u32[]{:S(2)}) collective-permute-start(f32[1,104,128]{2,1,0:T(8,128)S(1)} %invert.1), channel_id=1, source_target_pairs={{0,8},{4,12},{8,0},{12,4},{16,24},{20,28},{24,16},{28,20},{1,9},{5... | collective-permute-start | bytes 159752 | tf_op jit(solution)/shard_map/ppermute | solution.py:345
  29.3 6.0 %collective-permute-start.9 = (f32[1,104,128]{2,1,0:T(8,128)S(1)}, f32[1,104,128]{2,1,0:T(8,128)S(1)}, u32[]{:S(2)}, u32[]{:S(2)}) collective-permute-start(f32[1,104,128]{2,1,0:T(8,128)S(1)} %invert.1), channel_id=1, source_target_pairs={{0,24},{4,28},{8,16},{12,20},{16,8},{20,12},{24,0},{28,4},{1,25},{... | collective-permute-start | bytes 159752 | tf_op jit(solution)/shard_map/ppermute | solution.py:345
  32.6 5.0 %collective-permute-start.8 = (f32[1,104,128]{2,1,0:T(8,128)S(1)}, f32[1,104,128]{2,1,0:T(8,128)S(1)}, u32[]{:S(2)}, u32[]{:S(2)}) collective-permute-start(f32[1,104,128]{2,1,0:T(8,128)S(1)} %invert.1), channel_id=1, source_target_pairs={{0,16},{4,20},{8,24},{12,28},{16,0},{20,4},{24,8},{28,12},{1,17},{... | collective-permute-start | bytes 159752 | tf_op jit(solution)/shard_map/ppermute | solution.py:345
  37.6 6.4 %collective-permute-start.10 = (f32[4,104,128]{2,1,0:T(8,128)S(1)}, f32[4,104,128]{2,1,0:T(8,128)S(1)}, u32[]{:S(2)}, u32[]{:S(2)}) collective-permute-start(f32[4,104,128]{2,1,0:T(8,128)S(1)} %pad_maximum_fusion.refs_0_), channel_id=1, source_target_pairs={{0,4},{4,0},{8,12},{12,8},{16,20},{20,16},{24,28},{28,24},{1,5},{5... | collective-permute-start | bytes 638984 | tf_op jit(solution)/shard_map/ppermute | solution.py:345
  38.2 6.8 %collective-permute-start.12 = (f32[4,104,128]{2,1,0:T(8,128)S(1)}, f32[4,104,128]{2,1,0:T(8,128)S(1)}, u32[]{:S(2)}, u32[]{:S(2)}) collective-permute-start(f32[4,104,128]{2,1,0:T(8,128)S(1)} %pad_maximum_fusion.refs_0_), channel_id=1, source_target_pairs={{0,2},{1,3},{2,0},{3,1},{4,6},{5,7},{6,4},{7,5},{8,10},{9,11},{10,... | collective-permute-start | bytes 638984 | tf_op jit(solution)/shard_map/ppermute | solution.py:345
  39.7 5.9 %collective-permute-start.15 = (f32[4,104,128]{2,1,0:T(8,128)S(1)}, f32[4,104,128]{2,1,0:T(8,128)S(1)}, u32[]{:S(2)}, u32[]{:S(2)}) collective-permute-start(f32[4,104,128]{2,1,0:T(8,128)S(1)} %pad_maximum_fusion.refs_0_), channel_id=1, source_target_pairs={{0,1},{1,0},{2,3},{3,2},{4,5},{5,4},{6,7},{7,6},{8,9},{9,8},{10,11... | collective-permute-start | bytes 638984 | tf_op jit(solution)/shard_map/ppermute | solution.py:345
  44.0 11.1 %collective-permute-start.14 = (f32[4,104,128]{2,1,0:T(8,128)S(1)}, f32[4,104,128]{2,1,0:T(8,128)S(1)}, u32[]{:S(2)}, u32[]{:S(2)}) collective-permute-start(f32[4,104,128]{2,1,0:T(8,128)S(1)} %collective-permute-done.10.refs_1_), channel_id=1, source_target_pairs={{0,2},{1,3},{2,0},{3,1},{4,6},{5,7},{6,4},{7,5},{8,10},{9,11},{10,... | collective-permute-start | bytes 638984 | tf_op jit(solution)/shard_map/ppermute | solution.py:345
  45.0 10.2 %collective-permute-start.11 = (f32[4,104,128]{2,1,0:T(8,128)S(1)}, f32[4,104,128]{2,1,0:T(8,128)S(1)}, u32[]{:S(2)}, u32[]{:S(2)}) collective-permute-start(f32[4,104,128]{2,1,0:T(8,128)S(1)} %collective-permute-done.10.refs_1_), channel_id=1, source_target_pairs={{0,1},{1,0},{2,3},{3,2},{4,5},{5,4},{6,7},{7,6},{8,9},{9,8},{10,11... | collective-permute-start | bytes 638984 | tf_op jit(solution)/shard_map/ppermute | solution.py:345
  45.0 10.2 %collective-permute-start.13 = (f32[4,104,128]{2,1,0:T(8,128)S(1)}, f32[4,104,128]{2,1,0:T(8,128)S(1)}, u32[]{:S(2)}, u32[]{:S(2)}) collective-permute-start(f32[4,104,128]{2,1,0:T(8,128)S(1)} %collective-permute-done.12.refs_2_), channel_id=1, source_target_pairs={{0,1},{1,0},{2,3},{3,2},{4,5},{5,4},{6,7},{7,6},{8,9},{9,8},{10,11... | collective-permute-start | bytes 638984 | tf_op jit(solution)/shard_map/ppermute | solution.py:345
  55.1 1.5 %collective-permute-start.16 = (f32[4,104,128]{2,1,0:T(8,128)S(1)}, f32[4,104,128]{2,1,0:T(8,128)S(1)}, u32[]{:S(2)}, u32[]{:S(2)}) collective-permute-start(f32[4,104,128]{2,1,0:T(8,128)S(1)} %collective-permute-done.14.refs_2_), channel_id=1, source_target_pairs={{0,1},{1,0},{2,3},{3,2},{4,5},{5,4},{6,7},{7,6},{8,9},{9,8},{10,11... | collective-permute-start | bytes 638984 | tf_op jit(solution)/shard_map/ppermute | solution.py:345

commit v5 on v4

--- a/solution.py
+++ b/solution.py
@@ -252,6 +252,11 @@
 
     def multiply(g):
         top_ref, mid_ref, end_ref = weights[3 * (g % 2) : 3 * (g % 2) + 3]
+
+        def last_tile(kept, end, here):
+            c = dot(end, end_ref[...], 1, 0)
+            buffer[g % 2, here, 512:640] = jnp.where(kept, c[:, :128] + c[:, 128:], 0.0)
+
         if g == 0:
             build(0, True, False)
         for part in range(parts):
@@ -269,9 +274,13 @@
             kept, right, end = keep[here], held[g][here, 128:640], held[g][here, 384:640]
             b = dot(jnp.concatenate([right, right], axis=1), mid_ref[...], 1, 0)
             buffer[g % 2, here, 256:512] = jnp.where(kept, b, 0.0)
-            c = dot(end, end_ref[...], 1, 0)
-            buffer[g % 2, here, 512:640] = jnp.where(kept, c[:, :128] + c[:, 128:], 0.0)
+            if g + 1 < n_groups:
+                last_tile(kept, end, here)
         copy(g, 1).start()
+        if g + 1 == n_groups:
+            for part in range(parts):
+                here = slice(part * rows // parts, (part + 1) * rows // parts)
+                last_tile(keep[here], held[g][here, 384:640], here)
         copy(g, 2).start()
 
     for arrival in incoming:

time: 68.2 us -> 68 us (level)
  transfers between devices with their start and end apart: 17 -> 17, of which waited for: 7 -> 7; matrix products, arithmetic and copies ran while one was open for 0% -> 0% of each run, Pallas kernels for 25% -> 24%
where the time goes in v5:
time: 68 us; the launch traced here: 67.8 us
  Pallas kernels  35.3 us (52%)
  starting transfers between devices  16.4 us (24%)
  waiting for transfers between devices  13.8 us (20%)
  local copies, waits for them, and re-layouts  1.19 us (2%)
  between operations  0.94 us (1%)
    pallas_call x3, Pallas kernels, apply(): pl.pallas_call(functools.partial(apply_kernel, first, n, fetched), out_sh...  24.7 us
    ppermute x17, starting transfers between devices, swap(): return lax.ppermute(x, axis, [(i, i ^ mask) for i in range(size)])  16.4 us
    ppermute x17, waiting for transfers between devices, swap(): return lax.ppermute(x, axis, [(i, i ^ mask) for i in range(size)])  13.8 us
    pallas_call x1, Pallas kernels, shards_small(): pl.pallas_call(invert_kernel, out_shape=jax.ShapeDtypeStruct((1, ROWS, MA...  6.99 us
    pallas_call x1, Pallas kernels, shards_small(): pl.pallas_call(fetch_kernel, out_shape=[jax.ShapeDtypeStruct((grad_rows.s...  2 us
  transfers between devices with their start and end apart: 17, of which 7 were waited for; matrix products, arithmetic and copies ran while one was open for 0% of the time, Pallas kernels for 24%

profile of v5, /device:TPU:0, one launch (start us, length us, event | category | flops | bytes accessed | tf_op | source)
XLA Modules:
  0.0 67.8 jit_solution(3684863091891739774)
XLA Ops:
  0.0 1.1 %copy-done = bf16[256,1280]{1,0:T(8,128)(2,1)S(1)} copy-done((bf16[256,1280]{1,0:T(8,128)(2,1)S(1)}, bf16[256,1280]{1,0:T(8,128)(2,1)}, u32[]{:S(2)}) %copy-start) | copy-done | bytes 655384
  1.1 0.7 %statistics_send.1 = (f32[4,104,128]{2,1,0:T(8,128)S(1)}, f32[8,128]{1,0:T(8,128)S(1)}) custom-call(bf16[256,1280]{1,0:T(8,128)(2,1)S(1)} %copy-done), custom_call_target="tpu_custom_call" | custom-call | tf_op jit(solution)/shard_map/statistics_send/pallas_call | solution.py:362
  1.8 3.0 %collective-permute-start = (f32[4,104,128]{2,1,0:T(8,128)S(1)}, f32[4,104,128]{2,1,0:T(8,128)S(1)}, u32[]{:S(2)}, u32[]{:S(2)}) collective-permute-start(f32[4,104,128]{2,1,0:T(8,128)S(1)} %get-tuple-element.25), channel_id=1, source_target_pairs={{0,4},{4,0},{8,12},{12,8},{16,20},{20,16},{24,28},{28,24},{1,5},{5... | collective-permute-start | bytes 638984 | tf_op jit(solution)/shard_map/ppermute | solution.py:354
  4.9 1.2 %collective-permute-done.1 = f32[8,128]{1,0:T(8,128)S(1)} collective-permute-done((f32[8,128]{1,0:T(8,128)S(1)}, f32[8,128]{1,0:T(8,128)S(1)}, u32[]{:S(2)}, u32[]{:S(2)}) %collective-permute-start.1) | collective-permute-done | bytes 4128 | tf_op jit(solution)/shard_map/ppermute | solution.py:354
  6.0 1.5 %collective-permute-start.2 = (f32[8,128]{1,0:T(8,128)S(1)}, f32[8,128]{1,0:T(8,128)S(1)}, u32[]{:S(2)}, u32[]{:S(2)}) collective-permute-start(f32[8,128]{1,0:T(8,128)S(1)} %add.58), channel_id=1, source_target_pairs={{0,2},{1,3},{2,0},{3,1},{4,6},{5,7},{6,4},{7,5},{8,10},{9,11},{10,... | collective-permute-start | bytes 12296 | tf_op jit(solution)/shard_map/ppermute | solution.py:354
  7.5 2.1 %collective-permute-done.2 = f32[8,128]{1,0:T(8,128)S(1)} collective-permute-done((f32[8,128]{1,0:T(8,128)S(1)}, f32[8,128]{1,0:T(8,128)S(1)}, u32[]{:S(2)}, u32[]{:S(2)}) %collective-permute-start.2) | collective-permute-done | bytes 4128 | tf_op jit(solution)/shard_map/ppermute | solution.py:354
  9.7 0.9 %statistics_keep.1 = f32[4,104,128]{2,1,0:T(8,128)S(1)} custom-call(bf16[256,1280]{1,0:T(8,128)(2,1)S(1)} %copy-done), custom_call_target="tpu_custom_call" | custom-call | tf_op jit(solution)/shard_map/statistics_keep/pallas_call | solution.py:371
  10.6 2.6 %collective-permute-done.3 = f32[8,128]{1,0:T(8,128)S(1)} collective-permute-done((f32[8,128]{1,0:T(8,128)S(1)}, f32[8,128]{1,0:T(8,128)S(1)}, u32[]{:S(2)}, u32[]{:S(2)}) %collective-permute-start.3) | collective-permute-done | bytes 4128 | tf_op jit(solution)/shard_map/ppermute | solution.py:354
  13.3 3.7 %collective-permute-start.6 = (f32[1,104,128]{2,1,0:T(8,128)S(1)}, f32[1,104,128]{2,1,0:T(8,128)S(1)}, u32[]{:S(2)}, u32[]{:S(2)}) collective-permute-start(f32[1,104,128]{2,1,0:T(8,128)S(1)} %get-tuple-element.33), channel_id=1, source_target_pairs={{0,24},{4,28},{8,16},{12,20},{16,8},{20,12},{24,0},{28,4},{1,25},{... | collective-permute-start | bytes 159752 | tf_op jit(solution)/shard_map/ppermute | solution.py:354
  17.0 0.8 %collective-permute-start.4 = (f32[1,104,128]{2,1,0:T(8,128)S(1)}, f32[1,104,128]{2,1,0:T(8,128)S(1)}, u32[]{:S(2)}, u32[]{:S(2)}) collective-permute-start(f32[1,104,128]{2,1,0:T(8,128)S(1)} %get-tuple-element.35), channel_id=1, source_target_pairs={{0,8},{4,12},{8,0},{12,4},{16,24},{20,28},{24,16},{28,20},{1,9},{5... | collective-permute-start | bytes 159752 | tf_op jit(solution)/shard_map/ppermute | solution.py:354
  17.8 1.6 %collective-permute-done.6.d_ref = f32[1,104,128]{2,1,0:T(8,128)S(1)} collective-permute-done((f32[1,104,128]{2,1,0:T(8,128)S(1)}, f32[1,104,128]{2,1,0:T(8,128)S(1)}, u32[]{:S(2)}, u32[]{:S(2)}) %collective-permute-start.6) | collective-permute-done | bytes 53280 | tf_op jit(solution)/shard_map/ppermute | solution.py:354
  19.4 2.6 %collective-permute-done.5.c_ref = f32[1,104,128]{2,1,0:T(8,128)S(1)} collective-permute-done((f32[1,104,128]{2,1,0:T(8,128)S(1)}, f32[1,104,128]{2,1,0:T(8,128)S(1)}, u32[]{:S(2)}, u32[]{:S(2)}) %collective-permute-start.5) | collective-permute-done | bytes 53280 | tf_op jit(solution)/shard_map/ppermute | solution.py:354
  22.0 7.0 %invert.1 = f32[1,104,128]{2,1,0:T(8,128)S(1)} custom-call(f32[1,104,128]{2,1,0:T(8,128)S(1)} %get-tuple-element.36.a_ref, f32[1,104,128]{2,1,0:T(8,128)S(1)} %collective-permute-done.4.b_ref, f32[1,104,128]{2,1,0:T(8,128)S(1)} %collective-permute-done.5.c_ref, f32[1,104,128]{2,1,0:T(8,128)S(1)} %collective-permute-done.6.d_ref), custom_call_target="tpu_custom_call" | custom-call | tf_op jit(solution)/shard_map/invert/pallas_call | solution.py:399
  29.3 3.2 %collective-permute-start.9 = (f32[1,104,128]{2,1,0:T(8,128)S(1)}, f32[1,104,128]{2,1,0:T(8,128)S(1)}, u32[]{:S(2)}, u32[]{:S(2)}) collective-permute-start(f32[1,104,128]{2,1,0:T(8,128)S(1)} %invert.1), channel_id=1, source_target_pairs={{0,24},{4,28},{8,16},{12,20},{16,8},{20,12},{24,0},{28,4},{1,25},{... | collective-permute-start | bytes 159752 | tf_op jit(solution)/shard_map/ppermute | solution.py:354
  33.3 2.0 %fetch.1.refs_1_ = bf16[1296,640]{1,0:T(8,128)(2,1)S(1)} custom-call(s32[11]{0:T(128)S(1)} %stack.43.at_ref, bf16[1296,5120]{1,0:T(8,128)(2,1)} %refs_4_.1), custom_call_target="tpu_custom_call" | custom-call | bytes 1658880 | tf_op jit(solution)/shard_map/fetch/pallas_call | solution.py:388
  35.3 2.3 %collective-permute-done.8 = f32[1,104,128]{2,1,0:T(8,128)S(1)} collective-permute-done((f32[1,104,128]{2,1,0:T(8,128)S(1)}, f32[1,104,128]{2,1,0:T(8,128)S(1)}, u32[]{:S(2)}, u32[]{:S(2)}) %collective-permute-start.8) | collective-permute-done | bytes 53280 | tf_op jit(solution)/shard_map/ppermute | solution.py:354
  37.6 0.6 collective-permute-start.10
  38.2 1.5 %collective-permute-start.12 = (f32[4,104,128]{2,1,0:T(8,128)S(1)}, f32[4,104,128]{2,1,0:T(8,128)S(1)}, u32[]{:S(2)}, u32[]{:S(2)}) collective-permute-start(f32[4,104,128]{2,1,0:T(8,128)S(1)} %pad_maximum_fusion.refs_0_), channel_id=1, source_target_pairs={{0,2},{1,3},{2,0},{3,1},{4,6},{5,7},{6,4},{7,5},{8,10},{9,11},{10,... | collective-permute-start | bytes 638984 | tf_op jit(solution)/shard_map/ppermute | solution.py:354
  39.7 4.2 %apply.3.refs_4_ = f32[1296,5120]{1,0:T(8,128)} custom-call(s32[11]{0:T(128)S(1)} %stack.43.at_ref, f32[4,104,128]{2,1,0:T(8,128)S(1)} %pad_maximum_fusion.refs_0_, bf16[1296,640]{1,0:T(8,128)(2,1)S(1)} %fetch.1.refs_1_), custom_call_target="tpu_custom_call" | custom-call | flops 849346560 | bytes 3317760 | tf_op jit(solution)/shard_map/apply/pallas_call | solution.py:320
  43.9 1.2 %collective-permute-start.14 = (f32[4,104,128]{2,1,0:T(8,128)S(1)}, f32[4,104,128]{2,1,0:T(8,128)S(1)}, u32[]{:S(2)}, u32[]{:S(2)}) collective-permute-start(f32[4,104,128]{2,1,0:T(8,128)S(1)} %collective-permute-done.10.refs_1_), channel_id=1, source_target_pairs={{0,2},{1,3},{2,0},{3,1},{4,6},{5,7},{6,4},{7,5},{8,10},{9,11},{10,... | collective-permute-start | bytes 638984 | tf_op jit(solution)/shard_map/ppermute | solution.py:354
  45.0 0.5 collective-permute-start.13
  45.5 9.5 %apply.4.refs_5_ = f32[1296,5120]{1,0:T(8,128)} custom-call(s32[11]{0:T(128)S(1)} %stack.43.at_ref, f32[4,104,128]{2,1,0:T(8,128)S(1)} %collective-permute-done.15.refs_0_, f32[4,104,128]{2,1,0:T(8,128)S(1)} %collective-permute-done.10.refs_1_, f32[4,104,128]{2,1,0:T(8,128)S(1)} %collective-permute-done.12.refs_2_, ...), custom_call_target="tpu_custom_call", output_to_operand_aliasing={{}: (5, {})} | custom-call | flops 2548039680 | bytes 9953280 | tf_op jit(solution)/shard_map/apply/pallas_call | solution.py:320
  55.1 1.4 %collective-permute-done.16.refs_3_ = f32[4,104,128]{2,1,0:T(8,128)S(1)} collective-permute-done((f32[4,104,128]{2,1,0:T(8,128)S(1)}, f32[4,104,128]{2,1,0:T(8,128)S(1)}, u32[]{:S(2)}, u32[]{:S(2)}) %collective-permute-start.16) | collective-permute-done | bytes 213024 | tf_op jit(solution)/shard_map/ppermute | solution.py:354
  56.5 11.1 %apply.5 = f32[1296,5120]{1,0:T(8,128)} custom-call(s32[11]{0:T(128)S(1)} %stack.43.at_ref, f32[4,104,128]{2,1,0:T(8,128)S(1)} %collective-permute-done.11.refs_0_, f32[4,104,128]{2,1,0:T(8,128)S(1)} %collective-permute-done.13.refs_1_, f32[4,104,128]{2,1,0:T(8,128)S(1)} %collective-permute-done.14.refs_2_, ...), custom_call_target="tpu_custom_call", output_to_operand_aliasing={{}: (6, {})} | custom-call | flops 3397386240 | bytes 13271040 | tf_op jit(solution)/shard_map/apply/pallas_call | solution.py:320
  (27 shorter events, 0.7 us)
Async XLA Ops:
  0.0 1.1 %copy-start = (bf16[256,1280]{1,0:T(8,128)(2,1)S(1)}, bf16[256,1280]{1,0:T(8,128)(2,1)}, u32[]{:S(2)}) copy-start(bf16[256,1280]{1,0:T(8,128)(2,1)} %act_ref.3) | copy-start | bytes 1966084
  1.8 11.4 %collective-permute-start = (f32[4,104,128]{2,1,0:T(8,128)S(1)}, f32[4,104,128]{2,1,0:T(8,128)S(1)}, u32[]{:S(2)}, u32[]{:S(2)}) collective-permute-start(f32[4,104,128]{2,1,0:T(8,128)S(1)} %get-tuple-element.25), channel_id=1, source_target_pairs={{0,4},{4,0},{8,12},{12,8},{16,20},{20,16},{24,28},{28,24},{1,5},{5... | collective-permute-start | bytes 638984 | tf_op jit(solution)/shard_map/ppermute | solution.py:354
  4.8 1.2 %collective-permute-start.1 = (f32[8,128]{1,0:T(8,128)S(1)}, f32[8,128]{1,0:T(8,128)S(1)}, u32[]{:S(2)}, u32[]{:S(2)}) collective-permute-start(f32[8,128]{1,0:T(8,128)S(1)} %get-tuple-element.26), channel_id=1, source_target_pairs={{0,1},{1,0},{2,3},{3,2},{4,5},{5,4},{6,7},{7,6},{8,9},{9,8},{10,11... | collective-permute-start | bytes 12296 | tf_op jit(solution)/shard_map/ppermute | solution.py:354
  6.0 3.6 %collective-permute-start.2 = (f32[8,128]{1,0:T(8,128)S(1)}, f32[8,128]{1,0:T(8,128)S(1)}, u32[]{:S(2)}, u32[]{:S(2)}) collective-permute-start(f32[8,128]{1,0:T(8,128)S(1)} %add.58), channel_id=1, source_target_pairs={{0,2},{1,3},{2,0},{3,1},{4,6},{5,7},{6,4},{7,5},{8,10},{9,11},{10,... | collective-permute-start | bytes 12296 | tf_op jit(solution)/shard_map/ppermute | solution.py:354
  9.6 3.6 %collective-permute-start.3 = (f32[8,128]{1,0:T(8,128)S(1)}, f32[8,128]{1,0:T(8,128)S(1)}, u32[]{:S(2)}, u32[]{:S(2)}) collective-permute-start(f32[8,128]{1,0:T(8,128)S(1)} %add.59), channel_id=1, source_target_pairs={{0,4},{4,0},{8,12},{12,8},{16,20},{20,16},{24,28},{28,24},{1,5},{5... | collective-permute-start | bytes 12296 | tf_op jit(solution)/shard_map/ppermute | solution.py:354
  13.3 6.1 %collective-permute-start.6 = (f32[1,104,128]{2,1,0:T(8,128)S(1)}, f32[1,104,128]{2,1,0:T(8,128)S(1)}, u32[]{:S(2)}, u32[]{:S(2)}) collective-permute-start(f32[1,104,128]{2,1,0:T(8,128)S(1)} %get-tuple-element.33), channel_id=1, source_target_pairs={{0,24},{4,28},{8,16},{12,20},{16,8},{20,12},{24,0},{28,4},{1,25},{... | collective-permute-start | bytes 159752 | tf_op jit(solution)/shard_map/ppermute | solution.py:354
  17.0 5.0 %collective-permute-start.5 = (f32[1,104,128]{2,1,0:T(8,128)S(1)}, f32[1,104,128]{2,1,0:T(8,128)S(1)}, u32[]{:S(2)}, u32[]{:S(2)}) collective-permute-start(f32[1,104,128]{2,1,0:T(8,128)S(1)} %get-tuple-element.34), channel_id=1, source_target_pairs={{0,16},{4,20},{8,24},{12,28},{16,0},{20,4},{24,8},{28,12},{1,17},{... | collective-permute-start | bytes 159752 | tf_op jit(solution)/shard_map/ppermute | solution.py:354
  17.0 5.0 %collective-permute-start.4 = (f32[1,104,128]{2,1,0:T(8,128)S(1)}, f32[1,104,128]{2,1,0:T(8,128)S(1)}, u32[]{:S(2)}, u32[]{:S(2)}) collective-permute-start(f32[1,104,128]{2,1,0:T(8,128)S(1)} %get-tuple-element.35), channel_id=1, source_target_pairs={{0,8},{4,12},{8,0},{12,4},{16,24},{20,28},{24,16},{28,20},{1,9},{5... | collective-permute-start | bytes 159752 | tf_op jit(solution)/shard_map/ppermute | solution.py:354
  29.0 6.3 %collective-permute-start.7 = (f32[1,104,128]{2,1,0:T(8,128)S(1)}, f32[1,104,128]{2,1,0:T(8,128)S(1)}, u32[]{:S(2)}, u32[]{:S(2)}) collective-permute-start(f32[1,104,128]{2,1,0:T(8,128)S(1)} %invert.1), channel_id=1, source_target_pairs={{0,8},{4,12},{8,0},{12,4},{16,24},{20,28},{24,16},{28,20},{1,9},{5... | collective-permute-start | bytes 159752 | tf_op jit(solution)/shard_map/ppermute | solution.py:354
  29.3 6.0 %collective-permute-start.9 = (f32[1,104,128]{2,1,0:T(8,128)S(1)}, f32[1,104,128]{2,1,0:T(8,128)S(1)}, u32[]{:S(2)}, u32[]{:S(2)}) collective-permute-start(f32[1,104,128]{2,1,0:T(8,128)S(1)} %invert.1), channel_id=1, source_target_pairs={{0,24},{4,28},{8,16},{12,20},{16,8},{20,12},{24,0},{28,4},{1,25},{... | collective-permute-start | bytes 159752 | tf_op jit(solution)/shard_map/ppermute | solution.py:354
  32.6 5.0 %collective-permute-start.8 = (f32[1,104,128]{2,1,0:T(8,128)S(1)}, f32[1,104,128]{2,1,0:T(8,128)S(1)}, u32[]{:S(2)}, u32[]{:S(2)}) collective-permute-start(f32[1,104,128]{2,1,0:T(8,128)S(1)} %invert.1), channel_id=1, source_target_pairs={{0,16},{4,20},{8,24},{12,28},{16,0},{20,4},{24,8},{28,12},{1,17},{... | collective-permute-start | bytes 159752 | tf_op jit(solution)/shard_map/ppermute | solution.py:354
  37.6 6.2 %collective-permute-start.10 = (f32[4,104,128]{2,1,0:T(8,128)S(1)}, f32[4,104,128]{2,1,0:T(8,128)S(1)}, u32[]{:S(2)}, u32[]{:S(2)}) collective-permute-start(f32[4,104,128]{2,1,0:T(8,128)S(1)} %pad_maximum_fusion.refs_0_), channel_id=1, source_target_pairs={{0,4},{4,0},{8,12},{12,8},{16,20},{20,16},{24,28},{28,24},{1,5},{5... | collective-permute-start | bytes 638984 | tf_op jit(solution)/shard_map/ppermute | solution.py:354
  38.2 6.8 %collective-permute-start.12 = (f32[4,104,128]{2,1,0:T(8,128)S(1)}, f32[4,104,128]{2,1,0:T(8,128)S(1)}, u32[]{:S(2)}, u32[]{:S(2)}) collective-permute-start(f32[4,104,128]{2,1,0:T(8,128)S(1)} %pad_maximum_fusion.refs_0_), channel_id=1, source_target_pairs={{0,2},{1,3},{2,0},{3,1},{4,6},{5,7},{6,4},{7,5},{8,10},{9,11},{10,... | collective-permute-start | bytes 638984 | tf_op jit(solution)/shard_map/ppermute | solution.py:354
  39.7 5.9 %collective-permute-start.15 = (f32[4,104,128]{2,1,0:T(8,128)S(1)}, f32[4,104,128]{2,1,0:T(8,128)S(1)}, u32[]{:S(2)}, u32[]{:S(2)}) collective-permute-start(f32[4,104,128]{2,1,0:T(8,128)S(1)} %pad_maximum_fusion.refs_0_), channel_id=1, source_target_pairs={{0,1},{1,0},{2,3},{3,2},{4,5},{5,4},{6,7},{7,6},{8,9},{9,8},{10,11... | collective-permute-start | bytes 638984 | tf_op jit(solution)/shard_map/ppermute | solution.py:354
  43.9 11.1 %collective-permute-start.14 = (f32[4,104,128]{2,1,0:T(8,128)S(1)}, f32[4,104,128]{2,1,0:T(8,128)S(1)}, u32[]{:S(2)}, u32[]{:S(2)}) collective-permute-start(f32[4,104,128]{2,1,0:T(8,128)S(1)} %collective-permute-done.10.refs_1_), channel_id=1, source_target_pairs={{0,2},{1,3},{2,0},{3,1},{4,6},{5,7},{6,4},{7,5},{8,10},{9,11},{10,... | collective-permute-start | bytes 638984 | tf_op jit(solution)/shard_map/ppermute | solution.py:354
  45.0 10.1 %collective-permute-start.11 = (f32[4,104,128]{2,1,0:T(8,128)S(1)}, f32[4,104,128]{2,1,0:T(8,128)S(1)}, u32[]{:S(2)}, u32[]{:S(2)}) collective-permute-start(f32[4,104,128]{2,1,0:T(8,128)S(1)} %collective-permute-done.10.refs_1_), channel_id=1, source_target_pairs={{0,1},{1,0},{2,3},{3,2},{4,5},{5,4},{6,7},{7,6},{8,9},{9,8},{10,11... | collective-permute-start | bytes 638984 | tf_op jit(solution)/shard_map/ppermute | solution.py:354
  45.0 10.1 %collective-permute-start.13 = (f32[4,104,128]{2,1,0:T(8,128)S(1)}, f32[4,104,128]{2,1,0:T(8,128)S(1)}, u32[]{:S(2)}, u32[]{:S(2)}) collective-permute-start(f32[4,104,128]{2,1,0:T(8,128)S(1)} %collective-permute-done.12.refs_2_), channel_id=1, source_target_pairs={{0,1},{1,0},{2,3},{3,2},{4,5},{5,4},{6,7},{7,6},{8,9},{9,8},{10,11... | collective-permute-start | bytes 638984 | tf_op jit(solution)/shard_map/ppermute | solution.py:354
  55.0 1.5 %collective-permute-start.16 = (f32[4,104,128]{2,1,0:T(8,128)S(1)}, f32[4,104,128]{2,1,0:T(8,128)S(1)}, u32[]{:S(2)}, u32[]{:S(2)}) collective-permute-start(f32[4,104,128]{2,1,0:T(8,128)S(1)} %collective-permute-done.14.refs_2_), channel_id=1, source_target_pairs={{0,1},{1,0},{2,3},{3,2},{4,5},{5,4},{6,7},{7,6},{8,9},{9,8},{10,11... | collective-permute-start | bytes 638984 | tf_op jit(solution)/shard_map/ppermute | solution.py:354
